TPU v7x, 32 devices: a whole 2x2x4 slice. The times are simulated.
32 devices in a mesh: dom: 8 (over z, x), slab: 4 (over y, core).
Axes of the slice: x: 2, y: 2, z: 4, core: 2. Of those that a mesh axis runs over, the one named last changes fastest.
Arguments:
- images: bfloat16 [512, 65536], P(('dom', 'slab')), may hold values from -11 to 11
- references: bfloat16 [16, 65536], P('dom'), may hold values from -6 to 6
- offsets: int32 [512, 2], P(('dom', 'slab')), may hold values from -8 to 8
- orientations: int32 [512, 2], P(('dom', 'slab')), may hold values from 0 to 15, as said below
- interp_mats: bfloat16 [8, 128, 128], replicated, may hold values from -0.5 to 0.5
- interp_index: int32 [512, 2], P(('dom', 'slab')), may hold values from 0 to 7
- owners: int32 [512, 512, 1], P(('dom', 'slab')), may hold values from 0 to 31; in each aligned block of 8192 rows (0 to 8191, 8192 to 16383, ..., all dimensions but the last counted through in order) at most 448 rows name the same one
- line_index: int32 [512, 512], P(('dom', 'slab')), may hold values from 0 to 2047
- volume_in: float32 [65536, 256], P(('dom', 'slab')), may hold values from -6 to 6
Outputs:
- volume: float32 [65536, 256], P(('dom', 'slab'))
- evidence: float32 [512], P(('dom', 'slab'))
Inputs may be any that keep to these rules, and one draw needn't show every extreme that they name: `orientations`: each particle lists 2 different projections. `owners`: among the rows of one device no owner is named more than 448 times, a bound that some block reaches.
All inputs are finite; a program needn't handle non-finite values.
Results may differ from a plain program's by a relative error of at most 0.0039.
Values may be sent and summed in bfloat16 or wider, within the bound.
No kernel may reach another device: no remote copies, remote signals or barrier semaphores. Data moves between devices by JAX's collectives and lax.ppermute only.
A program may use at most 192 MiB of HBM per device.

v0:
```python
import functools
import math

import jax
import jax.numpy as jnp
import numpy as np
from jax import lax
from jax.experimental import pallas as pl
from jax.experimental.pallas import tpu as pltpu
from jax.sharding import Mesh
from jax.sharding import PartitionSpec as P

FY = 256
FX = 128
TX = 4
TY = 4
LIST = 2
OFF = 8
INNER = 2
F32 = jnp.float32
BF16 = jnp.bfloat16
I32 = jnp.int32
STEP = 2.0 * math.pi / FY
SHIFTS = OFF + max(TX, TY) // 2
NSHIFT = 24


def vmem_params(mib):
    return pltpu.CompilerParams(vmem_limit_bytes=mib << 20)


def whole(shape):
    return pl.BlockSpec(shape, lambda *_: (0,) * len(shape))


def cost(flops, nbytes):
    return pl.CostEstimate(flops=int(flops), bytes_accessed=int(nbytes), transcendentals=0)


def iota(shape, axis):
    return lax.broadcasted_iota(I32, shape, axis)


def in_hbm(value):
    return pltpu.with_memory_space_constraint(value, pltpu.HBM)


def split(value):
    high = value.astype(BF16)
    return high, (value - high.astype(F32)).astype(BF16)


def slot_kernel(
    dests, group, pad, place_of, owner_ref, line_from, image_from,
    index_ref, digit_ref, real_ref, imag_ref, hot_ref, line_ref, image_ref, sems,
):
    number = owner_ref.shape[0]
    blocks = number * LIST
    planes = dests // group
    z = lax.axis_index("z")
    lines_in = pltpu.make_async_copy(line_from, line_ref, sems.at[0])
    lines_in.start()
    images_in = pltpu.make_async_copy(image_from, image_ref, sems.at[1])
    images_in.start()

    def widen(k, carry):
        for i in range(8):
            r = k * 8 + i
            at = pl.multiple_of(r * 2 * FX, 2 * FX)
            to = pl.ds(pl.multiple_of(r * number, number), number)
            real_ref[to, :] = image_ref[:, pl.ds(at, FX)].astype(F32)
            imag_ref[to, :] = image_ref[:, pl.ds(at + FX, FX)].astype(F32)
        return carry

    owner = owner_ref[...]
    plane = owner // group
    chunk = jnp.zeros_like(owner)
    for k in range(planes):
        at = functools.reduce(
            lambda value, p: jnp.where(z == p, int(place_of[p, k]), value), range(planes), 0
        )
        chunk = jnp.where(plane == k, at, chunk)
    dest = chunk * group + (owner & (group - 1))
    owner_rows = iota((dests, FY), 0)
    for b in range(blocks):
        n, l = b // LIST, b % LIST
        hot = owner_rows == dest[n : n + 1, l * FY : (l + 1) * FY]
        hot_ref[b * dests : (b + 1) * dests, :] = hot.astype(F32).astype(BF16)
    before = (iota((FY, FY), 0) < iota((FY, FY), 1)).astype(F32).astype(BF16)
    prefix = jnp.dot(hot_ref[...], before, preferred_element_type=F32)
    lines_in.wait()
    running = jnp.zeros((dests, 1), F32)
    lane = iota((1, FY), 1).astype(F32)
    ranks = iota((pad, FY), 0)
    total = jnp.zeros((4 * dests, pad), F32)
    for b in range(blocks):
        n, l = b // LIST, b % LIST
        hot = hot_ref[b * dests : (b + 1) * dests, :].astype(F32)
        part = prefix[b * dests : (b + 1) * dests, :]
        rank = jnp.sum(hot * (part + running), axis=0, keepdims=True).astype(I32)
        running = running + part[:, FY - 1 :] + hot[:, FY - 1 :]
        line = line_ref[n : n + 1, l * FY : (l + 1) * FY]
        digits = [
            hot * lane,
            hot * float(b),
            hot * (line & 255).astype(F32),
            hot * ((line >> 8) + 1).astype(F32),
        ]
        left = jnp.concatenate(digits, axis=0).astype(BF16)
        right = (ranks == rank).astype(F32).astype(BF16)
        total = total + lax.dot_general(
            left, right, (((1,), (1,)), ((), ())), preferred_element_type=F32
        )
    digit_ref[...] = total
    row = total[:dests].astype(I32) * number + (total[dests : 2 * dests].astype(I32) >> 1)
    index_ref[...] = jnp.where(iota((dests, pad), 1) == pad - 1, running.astype(I32), row)
    images_in.wait()
    lax.fori_loop(0, FY // 8, widen, 0)


def row_slots(place_of, owners, lines, images, dests, group, pad):
    number, width = images.shape
    return pl.pallas_call(
        functools.partial(slot_kernel, dests, group, pad, place_of),
        out_shape=(
            jax.ShapeDtypeStruct((dests, pad), I32),
            jax.ShapeDtypeStruct((4 * dests, pad), F32),
            pltpu.VMEM((number * FY, FX), F32),
            pltpu.VMEM((number * FY, FX), F32),
        ),
        in_specs=[pl.BlockSpec(memory_space=pltpu.VMEM)]
        + [pl.BlockSpec(memory_space=pltpu.HBM)] * 2,
        scratch_shapes=[
            pltpu.VMEM((number * LIST * dests, FY), BF16),
            pltpu.VMEM(lines.shape, I32),
            pltpu.VMEM(images.shape, BF16),
            pltpu.SemaphoreType.DMA((2,)),
        ],
        compiler_params=vmem_params(20),
        cost_estimate=cost(3e9, 12e6),
        name="slots",
    )(owners, in_hbm(lines), in_hbm(images))


def place_kernel(
    chunk, cap, index_ref, digit_ref, real_ref, imag_ref, out_ref, token_ref, left_ref, right_ref,
    held, sems,
):
    group, pad = index_ref.shape
    dests = digit_ref.shape[0] // 4
    words = pad // (2 * FX)
    span = cap + 16
    zeros = jnp.zeros((group * span, FX), F32)

    left_ref[...] = zeros
    right_ref[...] = zeros
    token_ref[...] = jnp.zeros_like(token_ref)
    def member(d, carry):
        start = d * span

        def some(i, inner):
            spots = [index_ref[d, i * 16 + j] for j in range(16)]
            lefts = [real_ref[pl.ds(at, 1), :] for at in spots]
            rights = [imag_ref[pl.ds(at, 1), :] for at in spots]
            for j in range(16):
                left_ref[pl.ds(start + i * 16 + j, 1), :] = lefts[j]
                right_ref[pl.ds(start + i * 16 + j, 1), :] = rights[j]
            return inner

        lax.fori_loop(0, (index_ref[d, pad - 1] + 15) // 16, some, 0)
        return carry

    lax.fori_loop(0, group, member, 0)
    copies = []
    for d in range(group):
        start = d * span
        for which in range(4):
            row = which * dests + chunk * group + d
            for word in range(words):
                to = start + cap + which * words + word
                lane = word * 2 * FX
                left_ref[to : to + 1, :] = digit_ref[row : row + 1, lane : lane + FX]
                right_ref[to : to + 1, :] = digit_ref[row : row + 1, lane + FX : lane + 2 * FX]
        at = slice(start, start + span)
        held[at, :FX] = left_ref[at, :].astype(BF16)
        held[at, FX:] = right_ref[at, :].astype(BF16)
        copies.append(pltpu.make_async_copy(held.at[at], out_ref.at[at], sems.at[d]))
        copies[-1].start()
    for copy in copies:
        copy.wait()


def placed_rows(chunk, group, cap, index, digits, real, imag):
    pad = index.shape[1]
    span = cap + 16
    vmem = pl.BlockSpec(memory_space=pltpu.VMEM)
    return pl.pallas_call(
        functools.partial(place_kernel, chunk, cap),
        grid=(1,),
        out_shape=(pltpu.HBM((group * span, 2 * FX), BF16), jax.ShapeDtypeStruct((8, FX), F32)),
        in_specs=[
            pl.BlockSpec((group, pad), lambda i: (chunk, 0), memory_space=pltpu.SMEM),
            vmem,
            vmem,
            vmem,
        ],
        out_specs=(pl.BlockSpec(memory_space=pltpu.HBM), vmem),
        scratch_shapes=[pltpu.VMEM((group * span, FX), F32)] * 2
        + [pltpu.VMEM((group * span, 2 * FX), BF16), pltpu.SemaphoreType.DMA((group,))],
        compiler_params=vmem_params(12),
        cost_estimate=cost(1e5, 1e5),
        name="place",
    )(index, digits, real, imag)


def rotate(real, imag, cosine, sine):
    return real * cosine - imag * sine, real * sine + imag * cosine


def score_kernel(
    planes, inner, half_ref, turn_ref, image_from, near_ref, far_ref, offset_ref, orient_ref,
    interp_ref, token_ref, table_ref, evidence_ref, image_ref, sems,
):
    number = image_ref.shape[0]
    refs = near_ref.shape[0]
    rows_half = FY // 2
    group = 16
    half = half_ref[0]
    copies = []
    for k in range(4):
        side = half if k < 2 else 1 - half
        quarter = FY * FX // 2
        at = pl.ds(pl.multiple_of((side * 2 + k % 2) * quarter, quarter), quarter)
        copies.append(
            pltpu.make_async_copy(image_from.at[:, at], image_ref.at[:, at], sems.at[k])
        )
        copies[-1].start()
    off_x = offset_ref[:, 0:1]
    off_y = offset_ref[:, 1:2]
    lane = iota((number, FX), 1)

    def wave(units):
        angle = STEP * (units & (FY - 1)).astype(F32)
        return jnp.cos(angle), jnp.sin(angle)

    col_cos, col_sin = wave(-lane * off_x)
    one_cos, one_sin = wave(jnp.broadcast_to(-off_y, (number, FX)))
    ref_lane = iota((1, FX), 1)
    x1_cos, x1_sin = wave(jnp.broadcast_to(ref_lane, (refs, FX)))
    x2_cos, x2_sin = wave(jnp.broadcast_to(2 * ref_lane, (refs, FX)))

    def shifts(real, imag, c1, s1, c2, s2):
        rc, rs, ic, is_ = real * c1, real * s1, imag * c1, imag * s1
        pairs = [
            (real * c2 + imag * s2, imag * c2 - real * s2),
            (rc + is_, ic - rs),
            (real, imag),
            (rc - is_, ic + rs),
        ]
        return pairs

    def stacked(pairs):
        return jnp.concatenate(
            [jnp.concatenate([p.astype(BF16), q.astype(BF16)], axis=1) for p, q in pairs],
            axis=0,
        )

    def run(ref, first, total, waits):
        start_cos, start_sin = wave(-(lane * off_x + first * off_y))

        def block(k, carry):
            total, cosine, sine = carry
            lefts, rights = [], []
            for i in range(group):
                r = first + k * group + i
                at = pl.multiple_of(r * 2 * FX, 2 * FX)
                at_ref = pl.multiple_of((k * group + i) * 2 * FX, 2 * FX)
                real = image_ref[:, pl.ds(at, FX)].astype(F32)
                imag = image_ref[:, pl.ds(at + FX, FX)].astype(F32)
                real, imag = rotate(real, imag, cosine, sine)
                cosine, sine = rotate(cosine, sine, one_cos, one_sin)
                lefts.append(
                    stacked(
                        shifts(
                            real, imag, turn_ref[0, r], turn_ref[1, r], turn_ref[2, r], turn_ref[3, r]
                        )
                    )
                )
                real = ref[:, pl.ds(at_ref, FX)].astype(F32)
                imag = ref[:, pl.ds(at_ref + FX, FX)].astype(F32)
                rights.append(stacked(shifts(real, imag, x1_cos, -x1_sin, x2_cos, -x2_sin)))
            total = total + lax.dot_general(
                jnp.concatenate(lefts, axis=1),
                jnp.concatenate(rights, axis=1),
                (((1,), (1,)), ((), ())),
                preferred_element_type=F32,
            )
            return total, cosine, sine

        carry = (total, start_cos, start_sin)
        turns = rows_half // group // len(waits)
        for k, wait in enumerate(waits):
            wait.wait()
            carry = lax.fori_loop(k * turns, (k + 1) * turns, block, carry)
        return carry[0]

    total = jnp.zeros((TY * number, TX * refs), F32)
    total = run(near_ref, half * rows_half, total, copies[:2])
    total = run(far_ref, (1 - half) * rows_half, total, copies[2:])
    total = total * (1.0 / math.sqrt(FY * 2 * FX))
    parts = [total[b * number : (b + 1) * number, :] for b in range(TY)]
    top = functools.reduce(jnp.maximum, parts)
    top = jnp.max(top, axis=1, keepdims=True)
    mass = sum(jnp.sum(jnp.exp(part - top), axis=1, keepdims=True) for part in parts)
    evidence = top + jnp.log(mass)
    evidence_ref[...] = jnp.broadcast_to(evidence, (number, FX))
    spot = iota((number, TX * refs), 1)
    shift_of = spot // refs
    spot = spot & (refs - 1)
    local = refs // (planes * inner)
    plane = lax.axis_index("z") - spot // (inner * local)
    plane = jnp.where(plane < 0, plane + planes, plane)
    column = lax.axis_index("x") ^ ((spot // local) & (inner - 1))
    name = (plane * inner + column) * local + (spot & (local - 1))
    slot = iota((number, FX), 1)
    table = jnp.where(slot == 32, off_x.astype(F32), 0.0)
    table = jnp.where(slot == 33, off_y.astype(F32), table)
    for l in range(LIST):
        table = jnp.where(slot == 34 + l, interp_ref[:, l : l + 1].astype(F32), table)
        for b in range(TY):
            weights = jnp.exp(parts[b] - evidence)
            for a in range(TX):
                chosen = (name == orient_ref[:, l : l + 1]) & (shift_of == a)
                value = jnp.sum(jnp.where(chosen, weights, 0.0), axis=1, keepdims=True)
                table = jnp.where(slot == l * 16 + b * TX + a, value, table)
    table_ref[...] = table


def weights_table(
    planes, inner, half, images, near, far, offsets, orientations, interp_index, token
):
    number = images.shape[0]
    turn = np.arange(FY) * STEP
    turns = np.stack([np.cos(turn), np.sin(turn), np.cos(2 * turn), np.sin(2 * turn)])
    smem = pl.BlockSpec(memory_space=pltpu.SMEM)
    vmem = pl.BlockSpec(memory_space=pltpu.VMEM)
    return pl.pallas_call(
        functools.partial(score_kernel, planes, inner),
        out_shape=[jax.ShapeDtypeStruct((number, FX), F32)] * 2,
        in_specs=[smem, smem, pl.BlockSpec(memory_space=pltpu.HBM)] + [vmem] * 6,
        scratch_shapes=[pltpu.VMEM(images.shape, BF16), pltpu.SemaphoreType.DMA((4,))],
        compiler_params=vmem_params(14),
        cost_estimate=cost(1e9, 5e6),
        name="scores",
    )(
        half, jnp.asarray(turns, F32), in_hbm(images), near, far, offsets, orientations,
        interp_index, token,
    )


def wave_table():
    shift = np.arange(NSHIFT)[:, None] - SHIFTS
    angle = STEP * ((shift * np.arange(FX)[None, :]) % FY)
    table = np.concatenate(
        [
            np.concatenate([np.cos(angle), np.sin(angle)], axis=1),
            np.concatenate([-np.sin(angle), np.cos(angle)], axis=1),
        ],
        axis=0,
    ).astype(np.float32)
    high = table.astype(jnp.bfloat16)
    low = (table - high.astype(np.float32)).astype(jnp.bfloat16)
    return np.concatenate([high, high, low], axis=0)


def gather_kernel(cap, pad, first, row_ref, table_ref, wave_ref, mats_ref, *refs):
    base_ref = refs[0] if first is None else None
    out_ref, mixed_ref, line_ref = refs[1 if first is None else 0], refs[-2], refs[-1]
    lines = out_ref.shape[0]
    members = table_ref.shape[0]
    count = mats_ref.shape[0]
    span = cap + 16
    group = row_ref.shape[0] // span
    words = pad // (2 * FX)
    low_count = count // 2
    table_high, table_low = split(table_ref[:, :64])
    picks = jnp.concatenate([table_high, table_low], axis=1)
    number = members // group
    mats = jnp.concatenate(
        [mats_ref[:low_count].reshape(low_count * FX, FX), mats_ref[low_count:].reshape(low_count * FX, FX)],
        axis=1,
    )
    def block(s, carry):
        at = pl.multiple_of(s * span, 16)
        extra = row_ref[pl.ds(at + cap, 16), :].astype(F32)
        digit = [
            jnp.concatenate(
                [extra[which * words + word : which * words + word + 1] for word in range(words)],
                axis=1,
            )[:, :cap].astype(I32)
            for which in range(4)
        ]
        r = digit[0]
        member = s * number + (digit[1] >> 1)
        front = (digit[1] & 1) == 0
        line_ref[s] = digit[2] + (digit[3] - 1) * 256
        hot = (iota((members, cap), 0) == member).astype(F32).astype(BF16)
        got = lax.dot_general(picks, hot, (((0,), (0,)), ((), ())), preferred_element_type=F32)
        got = got[:64] + got[64:]
        weight = jnp.where(front, got[0:16], got[16:32])
        off_x = got[32:33].astype(I32)
        off_y = got[33:34].astype(I32)
        interp = jnp.where(front, got[34:35], got[35:36])
        sub = iota((8, cap), 0)
        units = r * ((sub & 3) - TY // 2 - off_y) - jnp.where(sub >= 4, FY // 4, 0)
        wave = jnp.cos(STEP * (units & (FY - 1)).astype(F32))
        gate_real = sum(weight[b * TX : (b + 1) * TX] * wave[b : b + 1] for b in range(TY))
        gate_imag = sum(weight[b * TX : (b + 1) * TX] * wave[4 + b : 5 + b] for b in range(TY))
        spot = iota((NSHIFT, cap), 0) + off_x
        coef_real = jnp.zeros((NSHIFT, cap), F32)
        coef_imag = jnp.zeros((NSHIFT, cap), F32)
        for a in range(TX):
            here = spot == a - TX // 2 + SHIFTS
            coef_real = jnp.where(here, gate_real[a : a + 1], coef_real)
            coef_imag = jnp.where(here, gate_imag[a : a + 1], coef_imag)
        high, low = split(jnp.concatenate([coef_real, coef_imag], axis=0))
        coef = jnp.concatenate([high, low, high], axis=0)
        phase = lax.dot_general(
            coef, wave_ref[...], (((0,), (0,)), ((), ())), preferred_element_type=F32
        )
        values = row_ref[pl.ds(at, cap), :].astype(F32)
        real, imag = rotate(values[:, :FX], values[:, FX:], phase[:, :FX], phase[:, FX:])
        slices = jnp.concatenate([real, imag], axis=0).astype(BF16)
        column = jnp.transpose(jnp.broadcast_to(interp, (8, cap)))[:, 0:1]
        column = jnp.broadcast_to(column, (cap, FX)).astype(I32)
        column = jnp.concatenate([column, column], axis=0)
        which = jnp.where(column >= low_count, column - low_count, column)
        zero = jnp.zeros_like(slices)
        pieces = [jnp.where(which == q, slices, zero) for q in range(low_count)]
        mixed = jnp.dot(jnp.concatenate(pieces, axis=1), mats, preferred_element_type=F32)
        mixed = jnp.where(column >= low_count, mixed[:, FX:], mixed[:, :FX]).astype(BF16)
        to = pl.ds(pl.multiple_of(s * cap, 16), cap)
        mixed_ref[to, :FX] = mixed[:cap]
        mixed_ref[to, FX:] = mixed[cap:]
        return carry

    lax.fori_loop(0, group, block, 0, unroll=2 if first else 2)
    line = jnp.concatenate([line_ref[s] for s in range(group)], axis=1)
    tile = min(512, lines // 2)
    rows = iota((tile, group * cap), 0)
    for at in range(0, lines, tile):
        hot = jnp.where(rows == line - at, 1.0, 0.0).astype(BF16)
        value = jnp.dot(hot, mixed_ref[...], preferred_element_type=F32)
        if base_ref is not None:
            value = value + base_ref[at : at + tile, :]
        out_ref[at : at + tile, :] = value
        if first:
            refs[1][at : at + tile, :] = value.astype(BF16)


def partial_lines(cap, pad, rows, table, mats, lines, first, base=None):
    group = rows.shape[0] // (cap + 16)
    shape = jax.ShapeDtypeStruct((lines, 2 * FX), F32)
    short = jax.ShapeDtypeStruct((lines, 2 * FX), BF16)
    vmem = pl.BlockSpec(memory_space=pltpu.VMEM)
    extra = () if base is None else (base,)
    return pl.pallas_call(
        functools.partial(gather_kernel, cap, pad, None if extra else first),
        out_shape=(shape, short) if first else shape,
        in_specs=[vmem] * (4 + len(extra)),
        scratch_shapes=[
            pltpu.VMEM((group * cap, 2 * FX), BF16),
            pltpu.VMEM((group, 1, cap), I32),
        ],
        compiler_params=vmem_params(20),
        cost_estimate=cost(1e6, 1e5),
        name="lines",
    )(rows, table, jnp.asarray(wave_table()), mats, *extra)


def relay_kernel(planes, step, place_of, *refs):
    up_from, down_from, _, _, up_to, down_to, came_ref, sent_ref, sems = refs[-9:]
    parts = refs[:-9]
    z = lax.axis_index("z")
    lines = up_to.shape[0]
    tile = min(512, lines)
    tiles = lines // tile

    def pull(came, way, k):
        at = pl.ds(k * tile, tile)
        return pltpu.make_async_copy(came.at[at], came_ref.at[way, at], sems.at[0, way, k])

    def push(out, way, k):
        at = pl.ds(k * tile, tile)
        return pltpu.make_async_copy(sent_ref.at[way, at], out.at[at], sems.at[1, way, k])

    for p in range(planes):
        jobs = []
        if p < step:
            jobs.append((0, place_of[p, planes - step + p], up_from if p > 0 else None, up_to))
        if p >= planes - step:
            edge = p == planes - 1
            jobs.append((1, place_of[p, p - planes + step], None if edge else down_from, down_to))
        if jobs:

            @pl.when(z == p)
            def _(jobs=jobs):
                for way, _, came, _ in jobs:
                    for k in range(tiles if came is not None else 0):
                        pull(came, way, k).start()
                for way, index, came, out in jobs:
                    for k in range(tiles):
                        at = slice(k * tile, (k + 1) * tile)
                        value = parts[index][at, :]
                        if came is not None:
                            pull(came, way, k).wait()
                            value = value + came_ref[way, at, :].astype(F32)
                        sent_ref[way, at, :] = value.astype(BF16)
                        push(out, way, k).start()
                for way, _, _, out in jobs:
                    for k in range(tiles):
                        push(out, way, k).wait()


def relay(planes, step, place_of, parts, up, down, tokens):
    vmem = pl.BlockSpec(memory_space=pltpu.VMEM)
    hbm = pl.BlockSpec(memory_space=pltpu.HBM)
    lines = up.shape[0]
    return pl.pallas_call(
        functools.partial(relay_kernel, planes, step, place_of),
        out_shape=[pltpu.HBM(up.shape, BF16)] * 2,
        in_specs=[vmem] * len(parts) + [hbm, hbm, vmem, vmem],
        out_specs=[hbm, hbm],
        scratch_shapes=[
            pltpu.VMEM((2, lines, 2 * FX), BF16),
            pltpu.VMEM((2, lines, 2 * FX), BF16),
            pltpu.SemaphoreType.DMA((2, 2, lines // min(512, lines))),
        ],
        compiler_params=vmem_params(10),
        cost_estimate=cost(60e9, 8e6),
        name="relay",
    )(*parts, in_hbm(up), in_hbm(down), *tokens)


def together(*values):
    return lax.optimization_barrier(values)


def block_order(planes):
    return np.array(
        [sorted(range(planes), key=lambda d: (-abs(d - z), -d)) for z in range(planes)], np.int32
    )


def body(
    planes, inner, slab,
    images, references, offsets, orientations, interp_mats, interp_index, owners, line_index, volume_in,
):
    number = images.shape[0]
    lines = volume_in.shape[0]
    group = inner * slab
    devices = planes * group
    rows_all = number * LIST * FY
    cap = max(2, 7 * rows_all // (4 * devices))
    span = cap + 16
    pad = -(-(cap + 1) // (2 * FX)) * 2 * FX
    half = lax.axis_index("slab") % 2

    local = references.shape[0]
    width = references.shape[1]
    mine = lax.dynamic_slice_in_dim(references, half * (width // 2), width // 2, axis=1)
    block = [mine]
    for e in range(1, inner):
        block.append(lax.ppermute(mine, "x", [(i, i ^ e) for i in range(inner)]))

    place_of = np.argsort(block_order(planes), axis=1).astype(np.int32)
    index, digits, real, imag = row_slots(
        place_of,
        owners.reshape(number, LIST * FY),
        line_index,
        images,
        devices,
        group,
        pad,
    )
    block, index = together(block, index)
    block = jnp.concatenate(block, axis=0)
    near = [block]
    for shift in range(1, planes):
        near.append(lax.ppermute(block, "z", [(p, (p + shift) % planes) for p in range(planes)]))
    def place(k, index):
        return placed_rows(k, group, cap, index, digits, real, imag)

    placed = [None] * planes
    placed[0], token = place(0, index)
    token, index = together(token, index)
    placed[1], token = place(1, index)

    def to_members(value):
        return lax.all_to_all(
            value.reshape(group, span, 2 * FX), ("x", "slab"), 0, 0, tiled=True
        ).reshape(group * span, 2 * FX)

    got = to_members(placed[0])
    near, token = together(near, token)
    near = jnp.concatenate(near, axis=0)
    far = lax.ppermute(near, "slab", [(i, i ^ 1) for i in range(slab)])
    table, evidence = weights_table(
        planes, inner, half.reshape(1).astype(I32), images, near, far, offsets, orientations,
        interp_index, token,
    )
    table, got, index = together(table, got, index)
    early = min(2, planes - 1)
    placed[early], token = place(early, index)
    later = token
    tables = lax.all_to_all(
        jnp.broadcast_to(table[None], (group,) + table.shape), ("x", "slab"), 0, 0, tiled=True
    ).reshape(group * number, FX)
    tables, placed[1], later = together(tables, placed[1], later)
    got = [got, to_members(placed[1])]

    def lines_of(k, base=None):
        return partial_lines(cap, pad, got[k], tables, interp_mats, lines, k == 0, base)

    part, short = lines_of(0)
    part, index = together(part, index)
    parts = [part]
    for k in range(early + 1, min(early + 2, planes)):
        placed[k], token = place(k, index)
    placed[early], token = together(placed[early], token)
    got.append(to_members(placed[early]))
    up = down = lax.ppermute(short, "z", sorted({(0, 1), (planes - 1, planes - 2)}))
    for s in range(2, planes):
        part = lines_of(s - 1)
        if s + 1 < planes:
            part, index = together(part, index)
            if placed[s + 1] is None:
                placed[s + 1], _ = place(s + 1, index)
            part, placed[s + 1] = together(part, placed[s + 1])
            got.append(to_members(placed[s + 1]))
        parts.append(part)
        up_send, down_send = relay(planes, s, place_of, parts, up, down, (token, later))
        up = lax.ppermute(up_send, "z", [(p, p + 1) for p in range(s)])
        down = lax.ppermute(down_send, "z", [(p, p - 1) for p in range(planes - s, planes)])
    last = lines_of(planes - 1, volume_in)
    volume = last + up.astype(F32) + down.astype(F32)
    return volume, evidence[:, 0]


def solution(mesh):
    dom, slab = mesh.shape["dom"], mesh.shape["slab"]
    planes = dom // INNER
    fine = Mesh(mesh.devices.reshape(planes, INNER, slab), ("z", "x", "slab"))
    every = ("z", "x", "slab")
    in_specs = (
        P(every, None),
        P(("z", "x"), None),
        P(every, None),
        P(every, None),
        P(),
        P(every, None),
        P(every, None, None),
        P(every, None),
        P(every, None),
    )
    out_specs = (P(every, None), P(every))
    return jax.shard_map(
        functools.partial(body, planes, INNER, slab),
        mesh=fine,
        in_specs=in_specs,
        out_specs=out_specs,
        check_vma=False,
    )
```

profile of v0, /device:TPU:0, one launch (start us, length us, event | category | flops | bytes accessed | tf_op | source)
XLA Modules:
  0.0 184.7 jit_solution(2676329676164216871)
XLA Ops:
  1.7 3.0 %collective-permute-start = (bf16[2,32768]{1,0:T(2,128)(2,1)S(1)}, bf16[2,32768]{1,0:T(2,128)(2,1)S(1)}, u32[]{:S(2)}, u32[]{:S(2)}) collective-permute-start(bf16[2,32768]{1,0:T(2,128)(2,1)S(1)} %constant_dynamic-slice_fusion), channel_id=1, source_target_pairs={{0,4},{4,0},{1,5},{5,1},{2,6},{6,2},{3,7},{7,3},{8,12},{12,8},{9,1... | collective-permute-start | bytes 393224 | tf_op jit(solution)/shard_map/ppermute | solution.py:574
  5.4 4.7 %slots.1 = (s32[32,512]{1,0:T(8,128)S(1)}, f32[128,512]{1,0:T(8,128)S(1)}, f32[4096,128]{1,0:T(8,128)S(1)}, f32[4096,128]{1,0:T(8,128)S(1)}) custom-call(s32[16,512]{1,0:T(8,128)S(1)} %bitcast.19, s32[16,512]{1,0:T(8,128)} %line_from.1, bf16[16,65536]{1,0:T(8,128)(2,1)} %image_from.3), custom_call_target="tpu_custom_call" | custom-call | flops 3000000000 | bytes 12000000 | tf_op jit(solution)/shard_map/slots/pallas_call | solution.py:123
  10.4 1.6 collective-permute-start.1
  12.1 2.6 %collective-permute-start.2 = (bf16[4,32768]{1,0:T(4,128)(2,1)S(1)}, bf16[4,32768]{1,0:T(4,128)(2,1)S(1)}, u32[]{:S(2)}, u32[]{:S(2)}) collective-permute-start(bf16[4,32768]{1,0:T(4,128)(2,1)S(1)} %pad_maximum_fusion.1), channel_id=1, source_target_pairs={{0,16},{8,24},{16,0},{24,8},{1,17},{9,25},{17,1},{25,9},{2,18},{10... | collective-permute-start | bytes 786440 | tf_op jit(solution)/shard_map/ppermute | solution.py:590
  16.0 8.5 %place.5 = (bf16[3712,256]{1,0:T(8,128)(2,1)}, f32[8,128]{1,0:T(8,128)}) custom-call(s32[32,512]{1,0:T(8,128)S(1)} %get-tuple-element.65.index_ref, f32[128,512]{1,0:T(8,128)S(1)} %get-tuple-element.46.digit_ref, f32[4096,128]{1,0:T(8,128)S(1)} %get-tuple-element.47.real_ref, f32[4096,128]{1,0:T(8,128)S(1)} %get-tuple-element.48.imag_ref), custom_call_target="tpu_custom_call" | custom-call | flops 100000 | bytes 100000 | tf_op jit(solution)/shard_map/place/pallas_call | solution.py:197
  24.6 4.3 %all-to-all-start = ((bf16[8,464,256]{2,1,0:T(8,128)(2,1)}), bf16[8,464,256]{2,1,0:T(8,128)(2,1)}, u32[]{:S(2)}, u32[]{:S(2)}) async-start(bf16[8,464,256]{2,1,0:T(8,128)(2,1)} %bitcast.23), calls=%async_computation | async-start | bytes 3801088 | tf_op jit(solution)/shard_map/all_to_all | solution.py:600
  28.9 1.6 copy-done.2
  30.5 9.2 %place.4 = (bf16[3712,256]{1,0:T(8,128)(2,1)}, f32[8,128]{1,0:T(8,128)S(1)}) custom-call(s32[32,512]{1,0:T(8,128)S(1)} %get-tuple-element.65.index_ref, f32[128,512]{1,0:T(8,128)S(1)} %get-tuple-element.46.digit_ref, f32[4096,128]{1,0:T(8,128)S(1)} %get-tuple-element.47.real_ref, f32[4096,128]{1,0:T(8,128)S(1)} %copy-done.2), custom_call_target="tpu_custom_call" | custom-call | flops 100000 | bytes 100000 | tf_op jit(solution)/shard_map/place/pallas_call | solution.py:197
  39.8 2.5 %pad_maximum_fusion.near_ref = bf16[16,32768]{1,0:T(8,128)(2,1)} fusion(bf16[4,32768]{1,0:T(4,128)(2,1)} %collective-permute-done.3, bf16[4,32768]{1,0:T(4,128)(2,1)S(1)} %collective-permute-done.2, bf16[4,32768]{1,0:T(4,128)(2,1)S(1)} %collective-permute-done.1, bf16[4,32768]{1,0:T(4,128)(2,1)S(1)} %pad_maximum_fusion.1), kind=kLoop, calls=%fused_computation.1 | loop fusion | flops 4194304 | bytes 2097152 | tf_op jit(solution)/shard_map/concatenate | solution.py:606
  43.3 2.4 %collective-permute-done.4.far_ref = bf16[16,32768]{1,0:T(8,128)(2,1)} collective-permute-done((bf16[16,32768]{1,0:T(8,128)(2,1)}, bf16[16,32768]{1,0:T(8,128)(2,1)}, u32[]{:S(2)}, u32[]{:S(2)}) %collective-permute-start.4) | collective-permute-done | bytes 1048608 | tf_op jit(solution)/shard_map/ppermute | solution.py:607
  45.7 9.2 %scores.1 = (f32[16,128]{1,0:T(8,128)S(1)}, f32[16,128]{1,0:T(8,128)S(1)}) custom-call(s32[1]{0:T(128)} %bitcast.half_ref, f32[4,256]{1,0:T(4,128)S(1)} %copy-done.12, bf16[16,65536]{1,0:T(8,128)(2,1)} %image_from.3, bf16[16,32768]{1,0:T(8,128)(2,1)} %pad_maximum_fusion.near_ref, bf16[16,32768]{1,0:T(8,128)(2,1)} %collective-permute-done.4.far_ref, ...), custom_call_target="tpu_custom_call" | custom-call | flops 1000000000 | bytes 5000000 | tf_op jit(solution)/shard_map/scores/pallas_call | solution.py:347
  55.5 4.5 %all-to-all-start.1 = ((f32[8,16,128]{2,1,0:T(8,128)}), f32[8,16,128]{2,1,0:T(8,128)S(1)}, u32[]{:S(2)}, u32[]{:S(2)}) async-start(f32[8,16,128]{2,1,0:T(8,128)} %broadcast_in_dim.2), calls=%async_computation.1 | async-start | bytes 131072 | tf_op jit(solution)/shard_map/all_to_all | solution.py:616
  60.0 1.6 copy-done.3
  61.6 9.5 %place.6 = (bf16[3712,256]{1,0:T(8,128)(2,1)}, f32[8,128]{1,0:T(8,128)S(1)}) custom-call(s32[32,512]{1,0:T(8,128)S(1)} %get-tuple-element.65.index_ref, f32[128,512]{1,0:T(8,128)S(1)} %get-tuple-element.46.digit_ref, f32[4096,128]{1,0:T(8,128)S(1)} %get-tuple-element.47.real_ref, f32[4096,128]{1,0:T(8,128)S(1)} %copy-done.3), custom_call_target="tpu_custom_call" | custom-call | flops 100000 | bytes 100000 | tf_op jit(solution)/shard_map/place/pallas_call | solution.py:197
  71.1 4.7 %all-to-all-start.2 = ((bf16[8,464,256]{2,1,0:T(8,128)(2,1)}), bf16[8,464,256]{2,1,0:T(8,128)(2,1)}, u32[]{:S(2)}, u32[]{:S(2)}) async-start(bf16[8,464,256]{2,1,0:T(8,128)(2,1)} %bitcast.20), calls=%async_computation.2 | async-start | bytes 3801088 | tf_op jit(solution)/shard_map/all_to_all | solution.py:600
  75.8 13.5 %lines.5 = (f32[2048,256]{1,0:T(8,128)S(1)}, bf16[2048,256]{1,0:T(8,128)(2,1)}) custom-call(bf16[3712,256]{1,0:T(8,128)(2,1)} %bitcast.2.row_ref, f32[128,128]{1,0:T(8,128)S(1)} %bitcast.15, bf16[144,256]{1,0:T(8,128)(2,1)S(1)} %copy-done.11, bf16[8,128,128]{2,1,0:T(8,128)(2,1)S(1)} %copy-done.7), custom_call_target="tpu_custom_call" | custom-call | flops 1000000 | bytes 100000 | tf_op jit(solution)/shard_map/lines/pallas_call | solution.py:467
  89.3 2.7 %collective-permute-start.5 = (bf16[2048,256]{1,0:T(8,128)(2,1)}, bf16[2048,256]{1,0:T(8,128)(2,1)}, u32[]{:S(2)}, u32[]{:S(2)}) collective-permute-start(bf16[2048,256]{1,0:T(8,128)(2,1)} %get-tuple-element.74), channel_id=1, source_target_pairs={{0,8},{24,16},{1,9},{25,17},{2,10},{26,18},{3,11},{27,19},{4,12},{... | collective-permute-start | bytes 3145736 | tf_op jit(solution)/shard_map/ppermute | solution.py:632
  92.0 8.7 %place.7 = (bf16[3712,256]{1,0:T(8,128)(2,1)}, f32[8,128]{1,0:T(8,128)S(1)}) custom-call(s32[32,512]{1,0:T(8,128)S(1)} %get-tuple-element.65.index_ref, f32[128,512]{1,0:T(8,128)S(1)} %get-tuple-element.46.digit_ref, f32[4096,128]{1,0:T(8,128)S(1)} %get-tuple-element.47.real_ref, f32[4096,128]{1,0:T(8,128)S(1)} %copy-done.4), custom_call_target="tpu_custom_call" | custom-call | flops 100000 | bytes 100000 | tf_op jit(solution)/shard_map/place/pallas_call | solution.py:197
  100.8 4.6 %all-to-all-start.4 = ((bf16[8,464,256]{2,1,0:T(8,128)(2,1)}), bf16[8,464,256]{2,1,0:T(8,128)(2,1)S(1)}, u32[]{:S(2)}, u32[]{:S(2)}) async-start(bf16[8,464,256]{2,1,0:T(8,128)(2,1)} %bitcast.22), calls=%async_computation.4 | async-start | bytes 3801088 | tf_op jit(solution)/shard_map/all_to_all | solution.py:600
  105.4 12.5 %lines.4.refs_1_ = f32[2048,256]{1,0:T(8,128)S(1)} custom-call(bf16[3712,256]{1,0:T(8,128)(2,1)} %bitcast.5.row_ref, f32[128,128]{1,0:T(8,128)S(1)} %bitcast.16, bf16[144,256]{1,0:T(8,128)(2,1)S(1)} %copy-done.11, bf16[8,128,128]{2,1,0:T(8,128)(2,1)S(1)} %copy-done.7), custom_call_target="tpu_custom_call" | custom-call | flops 1000000 | bytes 100000 | tf_op jit(solution)/shard_map/lines/pallas_call | solution.py:467
  119.5 3.2 %collective-permute-start.6 = (bf16[2048,256]{1,0:T(8,128)(2,1)}, bf16[2048,256]{1,0:T(8,128)(2,1)}, u32[]{:S(2)}, u32[]{:S(2)}) collective-permute-start(bf16[2048,256]{1,0:T(8,128)(2,1)} %get-tuple-element.77), channel_id=1, source_target_pairs={{0,8},{8,16},{1,9},{9,17},{2,10},{10,18},{3,11},{11,19},{4,12},{12... | collective-permute-start | bytes 3145736 | tf_op jit(solution)/shard_map/ppermute | solution.py:643
  122.7 1.7 collective-permute-start.7
  124.4 4.5 %all-to-all-done.4 = bf16[8,464,256]{2,1,0:T(8,128)(2,1)S(1)} async-done(((bf16[8,464,256]{2,1,0:T(8,128)(2,1)}), bf16[8,464,256]{2,1,0:T(8,128)(2,1)S(1)}, u32[]{:S(2)}, u32[]{:S(2)}) %all-to-all-start.4) | async-done | bytes 1900576 | tf_op jit(solution)/shard_map/all_to_all | solution.py:600
  130.2 3.8 %all-to-all-start.3 = ((bf16[8,464,256]{2,1,0:T(8,128)(2,1)}), bf16[8,464,256]{2,1,0:T(8,128)(2,1)S(1)}, u32[]{:S(2)}, u32[]{:S(2)}) async-start(bf16[8,464,256]{2,1,0:T(8,128)(2,1)} %bitcast.21), calls=%async_computation.3 | async-start | bytes 3801088 | tf_op jit(solution)/shard_map/all_to_all | solution.py:600
  134.1 1.5 copy-done.6
  135.6 10.8 %lines.7.refs_2_ = f32[2048,256]{1,0:T(8,128)S(1)} custom-call(bf16[3712,256]{1,0:T(8,128)(2,1)S(1)} %bitcast.14, f32[128,128]{1,0:T(8,128)S(1)} %bitcast.17, bf16[144,256]{1,0:T(8,128)(2,1)S(1)} %copy-done.11, bf16[8,128,128]{2,1,0:T(8,128)(2,1)S(1)} %copy-done.7), custom_call_target="tpu_custom_call" | custom-call | flops 1000000 | bytes 100000 | tf_op jit(solution)/shard_map/lines/pallas_call | solution.py:467
  147.6 7.6 %collective-permute-start.8 = (bf16[2048,256]{1,0:T(8,128)(2,1)}, bf16[2048,256]{1,0:T(8,128)(2,1)}, u32[]{:S(2)}, u32[]{:S(2)}) collective-permute-start(bf16[2048,256]{1,0:T(8,128)(2,1)} %get-tuple-element.79), channel_id=1, source_target_pairs={{0,8},{8,16},{16,24},{1,9},{9,17},{17,25},{2,10},{10,18},{18,26},{... | collective-permute-start | bytes 3145736 | tf_op jit(solution)/shard_map/ppermute | solution.py:643
  157.4 1.6 copy-done.8
  158.9 10.8 %lines.6 = f32[2048,256]{1,0:T(8,128)S(1)} custom-call(bf16[3712,256]{1,0:T(8,128)(2,1)S(1)} %bitcast.13, f32[128,128]{1,0:T(8,128)S(1)} %bitcast.18, bf16[144,256]{1,0:T(8,128)(2,1)S(1)} %copy-done.11, bf16[8,128,128]{2,1,0:T(8,128)(2,1)S(1)} %copy-done.7, f32[2048,256]{1,0:T(8,128)S(1)} %copy-done.8), custom_call_target="tpu_custom_call" | custom-call | flops 1000000 | bytes 100000 | tf_op jit(solution)/shard_map/lines/pallas_call | solution.py:467
  169.8 6.7 %collective-permute-done.8 = bf16[2048,256]{1,0:T(8,128)(2,1)} collective-permute-done((bf16[2048,256]{1,0:T(8,128)(2,1)}, bf16[2048,256]{1,0:T(8,128)(2,1)}, u32[]{:S(2)}, u32[]{:S(2)}) %collective-permute-start.8) | collective-permute-done | bytes 1048608 | tf_op jit(solution)/shard_map/ppermute | solution.py:643
  176.4 5.1 %collective-permute-done.9 = bf16[2048,256]{1,0:T(8,128)(2,1)} collective-permute-done((bf16[2048,256]{1,0:T(8,128)(2,1)}, bf16[2048,256]{1,0:T(8,128)(2,1)}, u32[]{:S(2)}, u32[]{:S(2)}) %collective-permute-start.9) | collective-permute-done | bytes 1048608 | tf_op jit(solution)/shard_map/ppermute | solution.py:644
  181.6 3.1 %convert_add_fusion = f32[2048,256]{1,0:T(8,128)} fusion(bf16[2048,256]{1,0:T(8,128)(2,1)} %collective-permute-done.9, f32[2048,256]{1,0:T(8,128)S(1)} %lines.6, bf16[2048,256]{1,0:T(8,128)(2,1)} %collective-permute-done.8), kind=kLoop, calls=%fused_computation | loop fusion | flops 2097152 | bytes 6291456 | tf_op jit(solution)/shard_map/add | solution.py:646
  (58 shorter events, 11.4 us)
Async XLA Ops:
  1.7 8.5 %collective-permute-start = (bf16[2,32768]{1,0:T(2,128)(2,1)S(1)}, bf16[2,32768]{1,0:T(2,128)(2,1)S(1)}, u32[]{:S(2)}, u32[]{:S(2)}) collective-permute-start(bf16[2,32768]{1,0:T(2,128)(2,1)S(1)} %constant_dynamic-slice_fusion), channel_id=1, source_target_pairs={{0,4},{4,0},{1,5},{5,1},{2,6},{6,2},{3,7},{7,3},{8,12},{12,8},{9,1... | collective-permute-start | bytes 393224 | tf_op jit(solution)/shard_map/ppermute | solution.py:574
  10.1 14.4 %copy-start.1 = (f32[4096,128]{1,0:T(8,128)}, f32[4096,128]{1,0:T(8,128)S(1)}, u32[]{:S(2)}) copy-start(f32[4096,128]{1,0:T(8,128)S(1)} %get-tuple-element.48.imag_ref) | copy-start | bytes 6291460
  10.4 29.3 %collective-permute-start.1 = (bf16[4,32768]{1,0:T(4,128)(2,1)S(1)}, bf16[4,32768]{1,0:T(4,128)(2,1)S(1)}, u32[]{:S(2)}, u32[]{:S(2)}) collective-permute-start(bf16[4,32768]{1,0:T(4,128)(2,1)S(1)} %pad_maximum_fusion.1), channel_id=1, source_target_pairs={{0,8},{8,16},{16,24},{24,0},{1,9},{9,17},{17,25},{25,1},{2,10},{10... | collective-permute-start | bytes 786440 | tf_op jit(solution)/shard_map/ppermute | solution.py:590
  12.1 27.7 %collective-permute-start.2 = (bf16[4,32768]{1,0:T(4,128)(2,1)S(1)}, bf16[4,32768]{1,0:T(4,128)(2,1)S(1)}, u32[]{:S(2)}, u32[]{:S(2)}) collective-permute-start(bf16[4,32768]{1,0:T(4,128)(2,1)S(1)} %pad_maximum_fusion.1), channel_id=1, source_target_pairs={{0,16},{8,24},{16,0},{24,8},{1,17},{9,25},{17,1},{25,9},{2,18},{10... | collective-permute-start | bytes 786440 | tf_op jit(solution)/shard_map/ppermute | solution.py:590
  14.6 25.1 %collective-permute-start.3 = (bf16[4,32768]{1,0:T(4,128)(2,1)S(1)}, bf16[4,32768]{1,0:T(4,128)(2,1)}, u32[]{:S(2)}, u32[]{:S(2)}) collective-permute-start(bf16[4,32768]{1,0:T(4,128)(2,1)S(1)} %pad_maximum_fusion.1), channel_id=1, source_target_pairs={{0,24},{8,0},{16,8},{24,16},{1,25},{9,1},{17,9},{25,17},{2,26},{10... | collective-permute-start | bytes 786440 | tf_op jit(solution)/shard_map/ppermute | solution.py:590
  24.6 30.3 %all-to-all-start = ((bf16[8,464,256]{2,1,0:T(8,128)(2,1)}), bf16[8,464,256]{2,1,0:T(8,128)(2,1)}, u32[]{:S(2)}, u32[]{:S(2)}) async-start(bf16[8,464,256]{2,1,0:T(8,128)(2,1)} %bitcast.23), calls=%async_computation | async-start | bytes 3801088 | tf_op jit(solution)/shard_map/all_to_all | solution.py:600
  28.9 1.6 copy-start.2
  39.7 3.4 %copy-start.16 = (s32[16,2]{0,1:T(2,128)S(1)}, s32[16,2]{0,1:T(2,128)}, u32[]{:S(2)}) copy-start(s32[16,2]{0,1:T(2,128)} %param.16) | copy-start | bytes 388
  39.7 3.4 %copy-start.17 = (s32[16,2]{0,1:T(2,128)S(1)}, s32[16,2]{0,1:T(2,128)}, u32[]{:S(2)}) copy-start(s32[16,2]{0,1:T(2,128)} %param.17) | copy-start | bytes 388
  39.7 3.5 %copy-start.18 = (s32[16,2]{0,1:T(2,128)S(1)}, s32[16,2]{0,1:T(2,128)}, u32[]{:S(2)}) copy-start(s32[16,2]{0,1:T(2,128)} %param.19) | copy-start | bytes 388
  39.7 6.0 %copy-start.12 = (f32[4,256]{1,0:T(4,128)S(1)}, f32[4,256]{1,0:T(4,128)}, u32[]{:S(2)}) copy-start(f32[4,256]{1,0:T(4,128)} %constant.26.clone.turn_ref) | copy-start | bytes 12292
  42.3 3.4 %collective-permute-start.4 = (bf16[16,32768]{1,0:T(8,128)(2,1)}, bf16[16,32768]{1,0:T(8,128)(2,1)}, u32[]{:S(2)}, u32[]{:S(2)}) collective-permute-start(bf16[16,32768]{1,0:T(8,128)(2,1)} %pad_maximum_fusion.near_ref), channel_id=1, source_target_pairs={{0,1},{1,0},{2,3},{3,2},{4,5},{5,4},{6,7},{7,6},{8,9},{9,8},{10,11... | collective-permute-start | bytes 3145736 | tf_op jit(solution)/shard_map/ppermute | solution.py:607
  55.5 15.6 %all-to-all-start.1 = ((f32[8,16,128]{2,1,0:T(8,128)}), f32[8,16,128]{2,1,0:T(8,128)S(1)}, u32[]{:S(2)}, u32[]{:S(2)}) async-start(f32[8,16,128]{2,1,0:T(8,128)} %broadcast_in_dim.2), calls=%async_computation.1 | async-start | bytes 131072 | tf_op jit(solution)/shard_map/all_to_all | solution.py:616
  60.0 1.6 copy-start.3
  71.1 4.7 %copy-start.7 = (bf16[8,128,128]{2,1,0:T(8,128)(2,1)S(1)}, bf16[8,128,128]{2,1,0:T(8,128)(2,1)}, u32[]{:S(2)}) copy-start(bf16[8,128,128]{2,1,0:T(8,128)(2,1)} %mats_ref.7) | copy-start | bytes 786436
  71.1 4.7 %copy-start.11 = (bf16[144,256]{1,0:T(8,128)(2,1)S(1)}, bf16[144,256]{1,0:T(8,128)(2,1)}, u32[]{:S(2)}) copy-start(bf16[144,256]{1,0:T(8,128)(2,1)} %constant.27.clone.wave_ref) | copy-start | bytes 221188
  71.1 29.6 %all-to-all-start.2 = ((bf16[8,464,256]{2,1,0:T(8,128)(2,1)}), bf16[8,464,256]{2,1,0:T(8,128)(2,1)}, u32[]{:S(2)}, u32[]{:S(2)}) async-start(bf16[8,464,256]{2,1,0:T(8,128)(2,1)} %bitcast.20), calls=%async_computation.2 | async-start | bytes 3801088 | tf_op jit(solution)/shard_map/all_to_all | solution.py:600
  75.8 16.2 %copy-start.4 = (f32[4096,128]{1,0:T(8,128)S(1)}, f32[4096,128]{1,0:T(8,128)}, u32[]{:S(2)}) copy-start(f32[4096,128]{1,0:T(8,128)} %copy-done.1) | copy-start | bytes 6291460
  89.3 11.4 %copy-start.13 = (f32[2048,256]{1,0:T(8,128)}, f32[2048,256]{1,0:T(8,128)S(1)}, u32[]{:S(2)}) copy-start(f32[2048,256]{1,0:T(8,128)S(1)} %get-tuple-element.69.refs_0_) | copy-start | bytes 6291460
  89.3 28.6 %collective-permute-start.5 = (bf16[2048,256]{1,0:T(8,128)(2,1)}, bf16[2048,256]{1,0:T(8,128)(2,1)}, u32[]{:S(2)}, u32[]{:S(2)}) collective-permute-start(bf16[2048,256]{1,0:T(8,128)(2,1)} %get-tuple-element.74), channel_id=1, source_target_pairs={{0,8},{24,16},{1,9},{25,17},{2,10},{26,18},{3,11},{27,19},{4,12},{... | collective-permute-start | bytes 3145736 | tf_op jit(solution)/shard_map/ppermute | solution.py:632
  100.8 28.2 %all-to-all-start.4 = ((bf16[8,464,256]{2,1,0:T(8,128)(2,1)}), bf16[8,464,256]{2,1,0:T(8,128)(2,1)S(1)}, u32[]{:S(2)}, u32[]{:S(2)}) async-start(bf16[8,464,256]{2,1,0:T(8,128)(2,1)} %bitcast.22), calls=%async_computation.4 | async-start | bytes 3801088 | tf_op jit(solution)/shard_map/all_to_all | solution.py:600
  105.4 12.5 %copy-start.14 = (f32[2048,256]{1,0:T(8,128)S(1)}, f32[2048,256]{1,0:T(8,128)}, u32[]{:S(2)}) copy-start(f32[2048,256]{1,0:T(8,128)} %copy-done.13) | copy-start | bytes 6291460
  117.9 1.7 copy-start.9
  119.5 26.9 %collective-permute-start.6 = (bf16[2048,256]{1,0:T(8,128)(2,1)}, bf16[2048,256]{1,0:T(8,128)(2,1)}, u32[]{:S(2)}, u32[]{:S(2)}) collective-permute-start(bf16[2048,256]{1,0:T(8,128)(2,1)} %get-tuple-element.77), channel_id=1, source_target_pairs={{0,8},{8,16},{1,9},{9,17},{2,10},{10,18},{3,11},{11,19},{4,12},{12... | collective-permute-start | bytes 3145736 | tf_op jit(solution)/shard_map/ppermute | solution.py:643
  122.7 23.7 %collective-permute-start.7 = (bf16[2048,256]{1,0:T(8,128)(2,1)}, bf16[2048,256]{1,0:T(8,128)(2,1)}, u32[]{:S(2)}, u32[]{:S(2)}) collective-permute-start(bf16[2048,256]{1,0:T(8,128)(2,1)} %get-tuple-element.78), channel_id=1, source_target_pairs={{16,8},{24,16},{17,9},{25,17},{18,10},{26,18},{19,11},{27,19},{20,... | collective-permute-start | bytes 3145736 | tf_op jit(solution)/shard_map/ppermute | solution.py:644
  130.2 27.1 %all-to-all-start.3 = ((bf16[8,464,256]{2,1,0:T(8,128)(2,1)}), bf16[8,464,256]{2,1,0:T(8,128)(2,1)S(1)}, u32[]{:S(2)}, u32[]{:S(2)}) async-start(bf16[8,464,256]{2,1,0:T(8,128)(2,1)} %bitcast.21), calls=%async_computation.3 | async-start | bytes 3801088 | tf_op jit(solution)/shard_map/all_to_all | solution.py:600
  134.1 1.5 copy-start.6
  135.6 10.8 %copy-start.10 = (f32[2048,256]{1,0:T(8,128)S(1)}, f32[2048,256]{1,0:T(8,128)}, u32[]{:S(2)}) copy-start(f32[2048,256]{1,0:T(8,128)} %copy-done.9) | copy-start | bytes 6291460
  135.6 10.9 %copy-start.15 = (f32[2048,256]{1,0:T(8,128)S(1)}, f32[2048,256]{1,0:T(8,128)}, u32[]{:S(2)}) copy-start(f32[2048,256]{1,0:T(8,128)} %copy-done.13) | copy-start | bytes 6291460
  147.6 28.8 %collective-permute-start.8 = (bf16[2048,256]{1,0:T(8,128)(2,1)}, bf16[2048,256]{1,0:T(8,128)(2,1)}, u32[]{:S(2)}, u32[]{:S(2)}) collective-permute-start(bf16[2048,256]{1,0:T(8,128)(2,1)} %get-tuple-element.79), channel_id=1, source_target_pairs={{0,8},{8,16},{16,24},{1,9},{9,17},{17,25},{2,10},{10,18},{18,26},{... | collective-permute-start | bytes 3145736 | tf_op jit(solution)/shard_map/ppermute | solution.py:643
  155.2 26.4 %collective-permute-start.9 = (bf16[2048,256]{1,0:T(8,128)(2,1)}, bf16[2048,256]{1,0:T(8,128)(2,1)}, u32[]{:S(2)}, u32[]{:S(2)}) collective-permute-start(bf16[2048,256]{1,0:T(8,128)(2,1)} %get-tuple-element.80), channel_id=1, source_target_pairs={{8,0},{16,8},{24,16},{9,1},{17,9},{25,17},{10,2},{18,10},{26,18},{... | collective-permute-start | bytes 3145736 | tf_op jit(solution)/shard_map/ppermute | solution.py:644
  157.4 1.6 copy-start.8
  (2 other events, 2.2 us)
where the time goes:
time: 185 us
  Pallas kernels  99.8 us (54%)
  starting transfers between devices  47.6 us (26%)
  waiting for transfers between devices  19 us (10%)
  local copies, waits for them, and re-layouts  11.3 us (6%)
  other arithmetic  5.93 us (3%)
    pallas_call x4, Pallas kernels, partial_lines(): pl.pallas_call(functools.partial(gather_kernel, cap, pad, None if extra e...  47.6 us
    pallas_call x4, Pallas kernels, placed_rows(): pl.pallas_call(functools.partial(place_kernel, chunk, cap), grid=(1,), ou...  35.9 us
    all_to_all x4, starting transfers between devices, to_members(): lax.all_to_all(value.reshape(group, span, 2 * FX), ('x', 'slab'), 0, 0, t...  17.4 us
    ppermute x2, starting transfers between devices, body(): up = lax.ppermute(up_send, 'z', [(p, p + 1) for p in range(s)])  10.7 us
    unnamed x42, local copies, waits for them, and re-layouts  9.99 us
    pallas_call x1, Pallas kernels, weights_table(): pl.pallas_call(functools.partial(score_kernel, planes, inner), out_shape=...  9.19 us
    ppermute x2, waiting for transfers between devices, body(): up = lax.ppermute(up_send, 'z', [(p, p + 1) for p in range(s)])  6.66 us
    ppermute x3, starting transfers between devices, body(): lax.ppermute(block, 'z', [(p, (p + shift) % planes) for p in range(planes)])  5.57 us
  transfers between devices with their start and end apart: 15, of which 5 were waited for; matrix products, arithmetic and copies ran while one was open for 2% of the time, Pallas kernels for 54%

commit v1 on v0

--- a/solution.py
+++ b/solution.py
@@ -146,7 +146,8 @@
     chunk, cap, index_ref, digit_ref, real_ref, imag_ref, out_ref, token_ref, left_ref, right_ref,
     held, sems,
 ):
-    group, pad = index_ref.shape
+    group = out_ref.shape[0] // (cap + 16)
+    pad = index_ref.shape[0] // group
     dests = digit_ref.shape[0] // 4
     words = pad // (2 * FX)
     span = cap + 16
@@ -157,17 +158,20 @@
     token_ref[...] = jnp.zeros_like(token_ref)
     def member(d, carry):
         start = d * span
+        base = d * pad
 
         def some(i, inner):
-            spots = [index_ref[d, i * 16 + j] for j in range(16)]
-            lefts = [real_ref[pl.ds(at, 1), :] for at in spots]
-            rights = [imag_ref[pl.ds(at, 1), :] for at in spots]
-            for j in range(16):
-                left_ref[pl.ds(start + i * 16 + j, 1), :] = lefts[j]
-                right_ref[pl.ds(start + i * 16 + j, 1), :] = rights[j]
+            at = base + i * 32
+            to = start + i * 32
+            spots = [index_ref[at + j] for j in range(32)]
+            lefts = [real_ref[pl.ds(spot, 1), :] for spot in spots]
+            rights = [imag_ref[pl.ds(spot, 1), :] for spot in spots]
+            for j in range(32):
+                left_ref[pl.ds(to + j, 1), :] = lefts[j]
+                right_ref[pl.ds(to + j, 1), :] = rights[j]
             return inner
 
-        lax.fori_loop(0, (index_ref[d, pad - 1] + 15) // 16, some, 0)
+        lax.fori_loop(0, (index_ref[base + pad - 1] + 31) // 32, some, 0)
         return carry
 
     lax.fori_loop(0, group, member, 0)
@@ -191,7 +195,7 @@
 
 
 def placed_rows(chunk, group, cap, index, digits, real, imag):
-    pad = index.shape[1]
+    pad = digits.shape[1]
     span = cap + 16
     vmem = pl.BlockSpec(memory_space=pltpu.VMEM)
     return pl.pallas_call(
@@ -199,7 +203,7 @@
         grid=(1,),
         out_shape=(pltpu.HBM((group * span, 2 * FX), BF16), jax.ShapeDtypeStruct((8, FX), F32)),
         in_specs=[
-            pl.BlockSpec((group, pad), lambda i: (chunk, 0), memory_space=pltpu.SMEM),
+            pl.BlockSpec((group * pad,), lambda i: (chunk,), memory_space=pltpu.SMEM),
             vmem,
             vmem,
             vmem,
@@ -475,7 +479,7 @@
         compiler_params=vmem_params(20),
         cost_estimate=cost(1e6, 1e5),
         name="lines",
-    )(rows, table, jnp.asarray(wave_table()), mats, *extra)
+    )(in_hbm(rows), table, jnp.asarray(wave_table()), mats, *extra)
 
 
 def relay_kernel(planes, step, place_of, *refs):
@@ -588,6 +592,8 @@
     near = [block]
     for shift in range(1, planes):
         near.append(lax.ppermute(block, "z", [(p, (p + shift) % planes) for p in range(planes)]))
+    index = index.reshape(devices * pad)
+
     def place(k, index):
         return placed_rows(k, group, cap, index, digits, real, imag)
 

time: 185 us -> 177 us (0.957)
  Pallas kernels: 99.8 us -> 88.6 us
  starting transfers between devices: 47.6 us -> 53.5 us
  local copies, waits for them, and re-layouts: 11.3 us -> 6.97 us
    pallas_call x4, Pallas kernels: 35.9 us -> 21.5 us  [placed_rows(): pl.pallas_call(functools.partial(place_kernel, chunk, cap), grid=(1,), ou...]
    unnamed x42 -> x39, local copies, waits for them, and re-layouts: 9.99 us -> 5.63 us
    ppermute x2, starting transfers between devices: 10.7 us -> 14.3 us  [body(): up = lax.ppermute(up_send, 'z', [(p, p + 1) for p in range(s)])]
    ppermute x1, starting transfers between devices: 2.7 us -> 6.12 us  [body(): lax.ppermute(short, 'z', sorted({(0, 1), (planes - 1, planes - 2)}))]
    pallas_call x4, Pallas kernels: 47.6 us -> 50.9 us  [partial_lines(): pl.pallas_call(functools.partial(gather_kernel, cap, pad, None if extra e...]
    ppermute x2, waiting for transfers between devices: 6.66 us -> 8.62 us  [body(): up = lax.ppermute(up_send, 'z', [(p, p + 1) for p in range(s)])]
  transfers between devices with their start and end apart: 15 -> 15, of which waited for: 5 -> 6; matrix products, arithmetic and copies ran while one was open for 2% -> 2% of each run, Pallas kernels for 54% -> 50%
where the time goes in v1:
time: 177 us; the launch traced here: 176 us
  Pallas kernels  88.6 us (50%)
  starting transfers between devices  53.5 us (30%)
  waiting for transfers between devices  20.1 us (11%)
  local copies, waits for them, and re-layouts  6.97 us (4%)
  other arithmetic  6.03 us (3%)
    pallas_call x4, Pallas kernels, partial_lines(): pl.pallas_call(functools.partial(gather_kernel, cap, pad, None if extra e...  50.9 us
    pallas_call x4, Pallas kernels, placed_rows(): pl.pallas_call(functools.partial(place_kernel, chunk, cap), grid=(1,), ou...  21.5 us
    all_to_all x4, starting transfers between devices, to_members(): lax.all_to_all(value.reshape(group, span, 2 * FX), ('x', 'slab'), 0, 0, t...  17.9 us
    ppermute x2, starting transfers between devices, body(): up = lax.ppermute(up_send, 'z', [(p, p + 1) for p in range(s)])  14.3 us
    pallas_call x1, Pallas kernels, weights_table(): pl.pallas_call(functools.partial(score_kernel, planes, inner), out_shape=...  9.19 us
    ppermute x2, waiting for transfers between devices, body(): up = lax.ppermute(up_send, 'z', [(p, p + 1) for p in range(s)])  8.62 us
    ppermute x1, starting transfers between devices, body(): lax.ppermute(short, 'z', sorted({(0, 1), (planes - 1, planes - 2)}))  6.12 us
    unnamed x39, local copies, waits for them, and re-layouts  5.63 us
  transfers between devices with their start and end apart: 15, of which 6 were waited for; matrix products, arithmetic and copies ran while one was open for 2% of the time, Pallas kernels for 50%

profile of v1, /device:TPU:0, one launch (start us, length us, event | category | flops | bytes accessed | tf_op | source)
XLA Modules:
  0.0 176.2 jit_solution(10052768105570511090)
XLA Ops:
  1.7 3.0 %collective-permute-start = (bf16[2,32768]{1,0:T(2,128)(2,1)S(1)}, bf16[2,32768]{1,0:T(2,128)(2,1)S(1)}, u32[]{:S(2)}, u32[]{:S(2)}) collective-permute-start(bf16[2,32768]{1,0:T(2,128)(2,1)S(1)} %constant_dynamic-slice_fusion), channel_id=1, source_target_pairs={{0,4},{4,0},{1,5},{5,1},{2,6},{6,2},{3,7},{7,3},{8,12},{12,8},{9,1... | collective-permute-start | bytes 393224 | tf_op jit(solution)/shard_map/ppermute | solution.py:578
  5.4 4.7 %slots.1 = (s32[32,512]{1,0:T(8,128)S(1)}, f32[128,512]{1,0:T(8,128)S(1)}, f32[4096,128]{1,0:T(8,128)S(1)}, f32[4096,128]{1,0:T(8,128)S(1)}) custom-call(s32[16,512]{1,0:T(8,128)S(1)} %bitcast.24, s32[16,512]{1,0:T(8,128)} %line_from.1, bf16[16,65536]{1,0:T(8,128)(2,1)} %image_from.3), custom_call_target="tpu_custom_call" | custom-call | flops 3000000000 | bytes 12000000 | tf_op jit(solution)/shard_map/slots/pallas_call | solution.py:123
  10.4 1.6 collective-permute-start.1
  12.1 2.6 %collective-permute-start.2 = (bf16[4,32768]{1,0:T(4,128)(2,1)S(1)}, bf16[4,32768]{1,0:T(4,128)(2,1)}, u32[]{:S(2)}, u32[]{:S(2)}) collective-permute-start(bf16[4,32768]{1,0:T(4,128)(2,1)S(1)} %pad_maximum_fusion.1), channel_id=1, source_target_pairs={{0,16},{8,24},{16,0},{24,8},{1,17},{9,25},{17,1},{25,9},{2,18},{10... | collective-permute-start | bytes 786440 | tf_op jit(solution)/shard_map/ppermute | solution.py:594
  16.0 5.5 %place.5 = (bf16[3712,256]{1,0:T(8,128)(2,1)}, f32[8,128]{1,0:T(8,128)}) custom-call(s32[16384]{0:T(1024)S(1)} %bitcast.15, f32[128,512]{1,0:T(8,128)S(1)} %get-tuple-element.46.digit_ref, f32[4096,128]{1,0:T(8,128)S(1)} %get-tuple-element.47.real_ref, f32[4096,128]{1,0:T(8,128)S(1)} %get-tuple-element.48.imag_ref), custom_call_target="tpu_custom_call" | custom-call | flops 100000 | bytes 100000 | tf_op jit(solution)/shard_map/place/pallas_call | solution.py:201
  21.6 4.3 %all-to-all-start = ((bf16[8,464,256]{2,1,0:T(8,128)(2,1)}), bf16[8,464,256]{2,1,0:T(8,128)(2,1)}, u32[]{:S(2)}, u32[]{:S(2)}) async-start(bf16[8,464,256]{2,1,0:T(8,128)(2,1)} %bitcast.28), calls=%async_computation | async-start | bytes 3801088 | tf_op jit(solution)/shard_map/all_to_all | solution.py:606
  25.9 1.6 copy-done.2
  27.5 5.2 %place.4 = (bf16[3712,256]{1,0:T(8,128)(2,1)}, f32[8,128]{1,0:T(8,128)S(1)}) custom-call(s32[16384]{0:T(1024)S(1)} %bitcast.16, f32[128,512]{1,0:T(8,128)S(1)} %get-tuple-element.46.digit_ref, f32[4096,128]{1,0:T(8,128)S(1)} %get-tuple-element.47.real_ref, f32[4096,128]{1,0:T(8,128)S(1)} %copy-done.2), custom_call_target="tpu_custom_call" | custom-call | flops 100000 | bytes 100000 | tf_op jit(solution)/shard_map/place/pallas_call | solution.py:201
  32.8 2.6 %pad_maximum_fusion.near_ref = bf16[16,32768]{1,0:T(8,128)(2,1)} fusion(bf16[4,32768]{1,0:T(4,128)(2,1)} %collective-permute-done.3, bf16[4,32768]{1,0:T(4,128)(2,1)} %collective-permute-done.2, bf16[4,32768]{1,0:T(4,128)(2,1)S(1)} %collective-permute-done.1, bf16[4,32768]{1,0:T(4,128)(2,1)S(1)} %pad_maximum_fusion.1), kind=kLoop, calls=%fused_computation.1 | loop fusion | flops 4194304 | bytes 2097152 | tf_op jit(solution)/shard_map/concatenate | solution.py:612
  36.0 2.4 %collective-permute-done.4.far_ref = bf16[16,32768]{1,0:T(8,128)(2,1)} collective-permute-done((bf16[16,32768]{1,0:T(8,128)(2,1)}, bf16[16,32768]{1,0:T(8,128)(2,1)}, u32[]{:S(2)}, u32[]{:S(2)}) %collective-permute-start.4) | collective-permute-done | bytes 1048608 | tf_op jit(solution)/shard_map/ppermute | solution.py:613
  38.4 9.2 %scores.1 = (f32[16,128]{1,0:T(8,128)S(1)}, f32[16,128]{1,0:T(8,128)S(1)}) custom-call(s32[1]{0:T(128)} %bitcast.half_ref, f32[4,256]{1,0:T(4,128)S(1)} %copy-done.10, bf16[16,65536]{1,0:T(8,128)(2,1)} %image_from.3, bf16[16,32768]{1,0:T(8,128)(2,1)} %pad_maximum_fusion.near_ref, bf16[16,32768]{1,0:T(8,128)(2,1)} %collective-permute-done.4.far_ref, ...), custom_call_target="tpu_custom_call" | custom-call | flops 1000000000 | bytes 5000000 | tf_op jit(solution)/shard_map/scores/pallas_call | solution.py:351
  47.6 1.9 %all-to-all-done = bf16[8,464,256]{2,1,0:T(8,128)(2,1)} async-done(((bf16[8,464,256]{2,1,0:T(8,128)(2,1)}), bf16[8,464,256]{2,1,0:T(8,128)(2,1)}, u32[]{:S(2)}, u32[]{:S(2)}) %all-to-all-start) | async-done | bytes 1900576 | tf_op jit(solution)/shard_map/all_to_all | solution.py:606
  50.1 3.3 %all-to-all-start.1 = ((f32[8,16,128]{2,1,0:T(8,128)}), f32[8,16,128]{2,1,0:T(8,128)S(1)}, u32[]{:S(2)}, u32[]{:S(2)}) async-start(f32[8,16,128]{2,1,0:T(8,128)} %broadcast_in_dim.2), calls=%async_computation.1 | async-start | bytes 131072 | tf_op jit(solution)/shard_map/all_to_all | solution.py:622
  53.5 1.6 copy-done.3
  55.1 5.4 %place.6 = (bf16[3712,256]{1,0:T(8,128)(2,1)}, f32[8,128]{1,0:T(8,128)S(1)}) custom-call(s32[16384]{0:T(1024)S(1)} %bitcast.17, f32[128,512]{1,0:T(8,128)S(1)} %get-tuple-element.46.digit_ref, f32[4096,128]{1,0:T(8,128)S(1)} %get-tuple-element.47.real_ref, f32[4096,128]{1,0:T(8,128)S(1)} %copy-done.3), custom_call_target="tpu_custom_call" | custom-call | flops 100000 | bytes 100000 | tf_op jit(solution)/shard_map/place/pallas_call | solution.py:201
  60.5 4.6 %all-to-all-start.2 = ((bf16[8,464,256]{2,1,0:T(8,128)(2,1)}), bf16[8,464,256]{2,1,0:T(8,128)(2,1)}, u32[]{:S(2)}, u32[]{:S(2)}) async-start(bf16[8,464,256]{2,1,0:T(8,128)(2,1)} %bitcast.25), calls=%async_computation.2 | async-start | bytes 3801088 | tf_op jit(solution)/shard_map/all_to_all | solution.py:606
  65.2 13.5 %lines.5 = (f32[2048,256]{1,0:T(8,128)S(1)}, bf16[2048,256]{1,0:T(8,128)(2,1)}) custom-call(bf16[3712,256]{1,0:T(8,128)(2,1)} %bitcast.2.row_ref, f32[128,128]{1,0:T(8,128)S(1)} %bitcast.19, bf16[144,256]{1,0:T(8,128)(2,1)S(1)} %copy-done.9, bf16[8,128,128]{2,1,0:T(8,128)(2,1)S(1)} %copy-done.5), custom_call_target="tpu_custom_call" | custom-call | flops 1000000 | bytes 100000 | tf_op jit(solution)/shard_map/lines/pallas_call | solution.py:471
  78.7 6.1 %collective-permute-start.5 = (bf16[2048,256]{1,0:T(8,128)(2,1)}, bf16[2048,256]{1,0:T(8,128)(2,1)}, u32[]{:S(2)}, u32[]{:S(2)}) collective-permute-start(bf16[2048,256]{1,0:T(8,128)(2,1)} %get-tuple-element.74), channel_id=1, source_target_pairs={{0,8},{24,16},{1,9},{25,17},{2,10},{26,18},{3,11},{27,19},{4,12},{... | collective-permute-start | bytes 3145736 | tf_op jit(solution)/shard_map/ppermute | solution.py:638
  84.8 5.4 %place.7 = (bf16[3712,256]{1,0:T(8,128)(2,1)}, f32[8,128]{1,0:T(8,128)S(1)}) custom-call(s32[16384]{0:T(1024)S(1)} %bitcast.18, f32[128,512]{1,0:T(8,128)S(1)} %get-tuple-element.46.digit_ref, f32[4096,128]{1,0:T(8,128)S(1)} %get-tuple-element.47.real_ref, f32[4096,128]{1,0:T(8,128)S(1)} %copy-done.4), custom_call_target="tpu_custom_call" | custom-call | flops 100000 | bytes 100000 | tf_op jit(solution)/shard_map/place/pallas_call | solution.py:201
  90.3 4.4 %all-to-all-start.4 = ((bf16[8,464,256]{2,1,0:T(8,128)(2,1)}), bf16[8,464,256]{2,1,0:T(8,128)(2,1)}, u32[]{:S(2)}, u32[]{:S(2)}) async-start(bf16[8,464,256]{2,1,0:T(8,128)(2,1)} %bitcast.27), calls=%async_computation.4 | async-start | bytes 3801088 | tf_op jit(solution)/shard_map/all_to_all | solution.py:606
  94.6 12.5 %lines.4.refs_1_ = f32[2048,256]{1,0:T(8,128)S(1)} custom-call(bf16[3712,256]{1,0:T(8,128)(2,1)} %bitcast.5.row_ref, f32[128,128]{1,0:T(8,128)S(1)} %bitcast.20, bf16[144,256]{1,0:T(8,128)(2,1)S(1)} %copy-done.9, bf16[8,128,128]{2,1,0:T(8,128)(2,1)S(1)} %copy-done.5), custom_call_target="tpu_custom_call" | custom-call | flops 1000000 | bytes 100000 | tf_op jit(solution)/shard_map/lines/pallas_call | solution.py:471
  108.8 5.7 %collective-permute-start.6 = (bf16[2048,256]{1,0:T(8,128)(2,1)}, bf16[2048,256]{1,0:T(8,128)(2,1)}, u32[]{:S(2)}, u32[]{:S(2)}) collective-permute-start(bf16[2048,256]{1,0:T(8,128)(2,1)} %get-tuple-element.77), channel_id=1, source_target_pairs={{0,8},{8,16},{1,9},{9,17},{2,10},{10,18},{3,11},{11,19},{4,12},{12... | collective-permute-start | bytes 3145736 | tf_op jit(solution)/shard_map/ppermute | solution.py:649
  114.5 1.6 collective-permute-start.7
  116.1 2.1 %all-to-all-done.4 = bf16[8,464,256]{2,1,0:T(8,128)(2,1)} async-done(((bf16[8,464,256]{2,1,0:T(8,128)(2,1)}), bf16[8,464,256]{2,1,0:T(8,128)(2,1)}, u32[]{:S(2)}, u32[]{:S(2)}) %all-to-all-start.4) | async-done | bytes 1900576 | tf_op jit(solution)/shard_map/all_to_all | solution.py:606
  118.2 4.5 %all-to-all-start.3 = ((bf16[8,464,256]{2,1,0:T(8,128)(2,1)}), bf16[8,464,256]{2,1,0:T(8,128)(2,1)}, u32[]{:S(2)}, u32[]{:S(2)}) async-start(bf16[8,464,256]{2,1,0:T(8,128)(2,1)} %bitcast.26), calls=%async_computation.3 | async-start | bytes 3801088 | tf_op jit(solution)/shard_map/all_to_all | solution.py:606
  122.8 12.5 %lines.7.refs_2_ = f32[2048,256]{1,0:T(8,128)S(1)} custom-call(bf16[3712,256]{1,0:T(8,128)(2,1)} %bitcast.9.row_ref, f32[128,128]{1,0:T(8,128)S(1)} %bitcast.21, bf16[144,256]{1,0:T(8,128)(2,1)S(1)} %copy-done.9, bf16[8,128,128]{2,1,0:T(8,128)(2,1)S(1)} %copy-done.5), custom_call_target="tpu_custom_call" | custom-call | flops 1000000 | bytes 100000 | tf_op jit(solution)/shard_map/lines/pallas_call | solution.py:471
  135.3 1.5 collective-permute-done.6.refs_3_
  137.9 8.6 %collective-permute-start.8 = (bf16[2048,256]{1,0:T(8,128)(2,1)}, bf16[2048,256]{1,0:T(8,128)(2,1)}, u32[]{:S(2)}, u32[]{:S(2)}) collective-permute-start(bf16[2048,256]{1,0:T(8,128)(2,1)} %get-tuple-element.79), channel_id=1, source_target_pairs={{0,8},{8,16},{16,24},{1,9},{9,17},{17,25},{2,10},{10,18},{18,26},{... | collective-permute-start | bytes 3145736 | tf_op jit(solution)/shard_map/ppermute | solution.py:649
  148.5 12.4 %lines.6 = f32[2048,256]{1,0:T(8,128)S(1)} custom-call(bf16[3712,256]{1,0:T(8,128)(2,1)} %bitcast.7.row_ref, f32[128,128]{1,0:T(8,128)S(1)} %bitcast.22, bf16[144,256]{1,0:T(8,128)(2,1)S(1)} %copy-done.9, bf16[8,128,128]{2,1,0:T(8,128)(2,1)S(1)} %copy-done.5, f32[2048,256]{1,0:T(8,128)S(1)} %copy-done.6), custom_call_target="tpu_custom_call" | custom-call | flops 1000000 | bytes 100000 | tf_op jit(solution)/shard_map/lines/pallas_call | solution.py:471
  160.8 7.2 %collective-permute-done.8 = bf16[2048,256]{1,0:T(8,128)(2,1)} collective-permute-done((bf16[2048,256]{1,0:T(8,128)(2,1)}, bf16[2048,256]{1,0:T(8,128)(2,1)}, u32[]{:S(2)}, u32[]{:S(2)}) %collective-permute-start.8) | collective-permute-done | bytes 1048608 | tf_op jit(solution)/shard_map/ppermute | solution.py:649
  168.0 5.1 %collective-permute-done.9 = bf16[2048,256]{1,0:T(8,128)(2,1)} collective-permute-done((bf16[2048,256]{1,0:T(8,128)(2,1)}, bf16[2048,256]{1,0:T(8,128)(2,1)}, u32[]{:S(2)}, u32[]{:S(2)}) %collective-permute-start.9) | collective-permute-done | bytes 1048608 | tf_op jit(solution)/shard_map/ppermute | solution.py:650
  173.1 3.1 %convert_add_fusion = f32[2048,256]{1,0:T(8,128)} fusion(bf16[2048,256]{1,0:T(8,128)(2,1)} %collective-permute-done.9, f32[2048,256]{1,0:T(8,128)S(1)} %lines.6, bf16[2048,256]{1,0:T(8,128)(2,1)} %collective-permute-done.8), kind=kLoop, calls=%fused_computation | loop fusion | flops 2097152 | bytes 6291456 | tf_op jit(solution)/shard_map/add | solution.py:652
  (55 shorter events, 9.5 us)
Async XLA Ops:
  0.6 1.0 copy-start
  1.7 8.5 %collective-permute-start = (bf16[2,32768]{1,0:T(2,128)(2,1)S(1)}, bf16[2,32768]{1,0:T(2,128)(2,1)S(1)}, u32[]{:S(2)}, u32[]{:S(2)}) collective-permute-start(bf16[2,32768]{1,0:T(2,128)(2,1)S(1)} %constant_dynamic-slice_fusion), channel_id=1, source_target_pairs={{0,4},{4,0},{1,5},{5,1},{2,6},{6,2},{3,7},{7,3},{8,12},{12,8},{9,1... | collective-permute-start | bytes 393224 | tf_op jit(solution)/shard_map/ppermute | solution.py:578
  10.1 11.4 %copy-start.1 = (f32[4096,128]{1,0:T(8,128)}, f32[4096,128]{1,0:T(8,128)S(1)}, u32[]{:S(2)}) copy-start(f32[4096,128]{1,0:T(8,128)S(1)} %get-tuple-element.48.imag_ref) | copy-start | bytes 6291460
  10.4 22.3 %collective-permute-start.1 = (bf16[4,32768]{1,0:T(4,128)(2,1)S(1)}, bf16[4,32768]{1,0:T(4,128)(2,1)S(1)}, u32[]{:S(2)}, u32[]{:S(2)}) collective-permute-start(bf16[4,32768]{1,0:T(4,128)(2,1)S(1)} %pad_maximum_fusion.1), channel_id=1, source_target_pairs={{0,8},{8,16},{16,24},{24,0},{1,9},{9,17},{17,25},{25,1},{2,10},{10... | collective-permute-start | bytes 786440 | tf_op jit(solution)/shard_map/ppermute | solution.py:594
  12.1 20.7 %collective-permute-start.2 = (bf16[4,32768]{1,0:T(4,128)(2,1)S(1)}, bf16[4,32768]{1,0:T(4,128)(2,1)}, u32[]{:S(2)}, u32[]{:S(2)}) collective-permute-start(bf16[4,32768]{1,0:T(4,128)(2,1)S(1)} %pad_maximum_fusion.1), channel_id=1, source_target_pairs={{0,16},{8,24},{16,0},{24,8},{1,17},{9,25},{17,1},{25,9},{2,18},{10... | collective-permute-start | bytes 786440 | tf_op jit(solution)/shard_map/ppermute | solution.py:594
  14.6 18.1 %collective-permute-start.3 = (bf16[4,32768]{1,0:T(4,128)(2,1)S(1)}, bf16[4,32768]{1,0:T(4,128)(2,1)}, u32[]{:S(2)}, u32[]{:S(2)}) collective-permute-start(bf16[4,32768]{1,0:T(4,128)(2,1)S(1)} %pad_maximum_fusion.1), channel_id=1, source_target_pairs={{0,24},{8,0},{16,8},{24,16},{1,25},{9,1},{17,9},{25,17},{2,26},{10... | collective-permute-start | bytes 786440 | tf_op jit(solution)/shard_map/ppermute | solution.py:594
  21.6 27.9 %all-to-all-start = ((bf16[8,464,256]{2,1,0:T(8,128)(2,1)}), bf16[8,464,256]{2,1,0:T(8,128)(2,1)}, u32[]{:S(2)}, u32[]{:S(2)}) async-start(bf16[8,464,256]{2,1,0:T(8,128)(2,1)} %bitcast.28), calls=%async_computation | async-start | bytes 3801088 | tf_op jit(solution)/shard_map/all_to_all | solution.py:606
  25.9 1.6 copy-start.2
  32.7 3.1 %copy-start.14 = (s32[16,2]{0,1:T(2,128)S(1)}, s32[16,2]{0,1:T(2,128)}, u32[]{:S(2)}) copy-start(s32[16,2]{0,1:T(2,128)} %param.16) | copy-start | bytes 388
  32.7 3.2 %copy-start.15 = (s32[16,2]{0,1:T(2,128)S(1)}, s32[16,2]{0,1:T(2,128)}, u32[]{:S(2)}) copy-start(s32[16,2]{0,1:T(2,128)} %param.17) | copy-start | bytes 388
  32.7 3.2 %copy-start.16 = (s32[16,2]{0,1:T(2,128)S(1)}, s32[16,2]{0,1:T(2,128)}, u32[]{:S(2)}) copy-start(s32[16,2]{0,1:T(2,128)} %param.19) | copy-start | bytes 388
  32.8 5.7 %copy-start.10 = (f32[4,256]{1,0:T(4,128)S(1)}, f32[4,256]{1,0:T(4,128)}, u32[]{:S(2)}) copy-start(f32[4,256]{1,0:T(4,128)} %constant.26.clone.turn_ref) | copy-start | bytes 12292
  35.4 3.0 %collective-permute-start.4 = (bf16[16,32768]{1,0:T(8,128)(2,1)}, bf16[16,32768]{1,0:T(8,128)(2,1)}, u32[]{:S(2)}, u32[]{:S(2)}) collective-permute-start(bf16[16,32768]{1,0:T(8,128)(2,1)} %pad_maximum_fusion.near_ref), channel_id=1, source_target_pairs={{0,1},{1,0},{2,3},{3,2},{4,5},{5,4},{6,7},{7,6},{8,9},{9,8},{10,11... | collective-permute-start | bytes 3145736 | tf_op jit(solution)/shard_map/ppermute | solution.py:613
  50.1 10.4 %all-to-all-start.1 = ((f32[8,16,128]{2,1,0:T(8,128)}), f32[8,16,128]{2,1,0:T(8,128)S(1)}, u32[]{:S(2)}, u32[]{:S(2)}) async-start(f32[8,16,128]{2,1,0:T(8,128)} %broadcast_in_dim.2), calls=%async_computation.1 | async-start | bytes 131072 | tf_op jit(solution)/shard_map/all_to_all | solution.py:622
  53.5 1.6 copy-start.3
  60.5 4.7 %copy-start.5 = (bf16[8,128,128]{2,1,0:T(8,128)(2,1)S(1)}, bf16[8,128,128]{2,1,0:T(8,128)(2,1)}, u32[]{:S(2)}) copy-start(bf16[8,128,128]{2,1,0:T(8,128)(2,1)} %mats_ref.7) | copy-start | bytes 786436
  60.5 4.7 %copy-start.9 = (bf16[144,256]{1,0:T(8,128)(2,1)S(1)}, bf16[144,256]{1,0:T(8,128)(2,1)}, u32[]{:S(2)}) copy-start(bf16[144,256]{1,0:T(8,128)(2,1)} %constant.27.clone.wave_ref) | copy-start | bytes 221188
  60.5 29.8 %all-to-all-start.2 = ((bf16[8,464,256]{2,1,0:T(8,128)(2,1)}), bf16[8,464,256]{2,1,0:T(8,128)(2,1)}, u32[]{:S(2)}, u32[]{:S(2)}) async-start(bf16[8,464,256]{2,1,0:T(8,128)(2,1)} %bitcast.25), calls=%async_computation.2 | async-start | bytes 3801088 | tf_op jit(solution)/shard_map/all_to_all | solution.py:606
  65.2 19.7 %copy-start.4 = (f32[4096,128]{1,0:T(8,128)S(1)}, f32[4096,128]{1,0:T(8,128)}, u32[]{:S(2)}) copy-start(f32[4096,128]{1,0:T(8,128)} %copy-done.1) | copy-start | bytes 6291460
  78.7 11.5 %copy-start.11 = (f32[2048,256]{1,0:T(8,128)}, f32[2048,256]{1,0:T(8,128)S(1)}, u32[]{:S(2)}) copy-start(f32[2048,256]{1,0:T(8,128)S(1)} %get-tuple-element.69.refs_0_) | copy-start | bytes 6291460
  78.7 28.4 %collective-permute-start.5 = (bf16[2048,256]{1,0:T(8,128)(2,1)}, bf16[2048,256]{1,0:T(8,128)(2,1)}, u32[]{:S(2)}, u32[]{:S(2)}) collective-permute-start(bf16[2048,256]{1,0:T(8,128)(2,1)} %get-tuple-element.74), channel_id=1, source_target_pairs={{0,8},{24,16},{1,9},{25,17},{2,10},{26,18},{3,11},{27,19},{4,12},{... | collective-permute-start | bytes 3145736 | tf_op jit(solution)/shard_map/ppermute | solution.py:638
  90.3 28.0 %all-to-all-start.4 = ((bf16[8,464,256]{2,1,0:T(8,128)(2,1)}), bf16[8,464,256]{2,1,0:T(8,128)(2,1)}, u32[]{:S(2)}, u32[]{:S(2)}) async-start(bf16[8,464,256]{2,1,0:T(8,128)(2,1)} %bitcast.27), calls=%async_computation.4 | async-start | bytes 3801088 | tf_op jit(solution)/shard_map/all_to_all | solution.py:606
  94.6 12.5 %copy-start.12 = (f32[2048,256]{1,0:T(8,128)S(1)}, f32[2048,256]{1,0:T(8,128)}, u32[]{:S(2)}) copy-start(f32[2048,256]{1,0:T(8,128)} %copy-done.11) | copy-start | bytes 6291460
  107.1 1.7 copy-start.7
  108.8 28.0 %collective-permute-start.6 = (bf16[2048,256]{1,0:T(8,128)(2,1)}, bf16[2048,256]{1,0:T(8,128)(2,1)}, u32[]{:S(2)}, u32[]{:S(2)}) collective-permute-start(bf16[2048,256]{1,0:T(8,128)(2,1)} %get-tuple-element.77), channel_id=1, source_target_pairs={{0,8},{8,16},{1,9},{9,17},{2,10},{10,18},{3,11},{11,19},{4,12},{12... | collective-permute-start | bytes 3145736 | tf_op jit(solution)/shard_map/ppermute | solution.py:649
  114.5 22.3 %collective-permute-start.7 = (bf16[2048,256]{1,0:T(8,128)(2,1)}, bf16[2048,256]{1,0:T(8,128)(2,1)}, u32[]{:S(2)}, u32[]{:S(2)}) collective-permute-start(bf16[2048,256]{1,0:T(8,128)(2,1)} %get-tuple-element.78), channel_id=1, source_target_pairs={{16,8},{24,16},{17,9},{25,17},{18,10},{26,18},{19,11},{27,19},{20,... | collective-permute-start | bytes 3145736 | tf_op jit(solution)/shard_map/ppermute | solution.py:650
  118.2 30.3 %all-to-all-start.3 = ((bf16[8,464,256]{2,1,0:T(8,128)(2,1)}), bf16[8,464,256]{2,1,0:T(8,128)(2,1)}, u32[]{:S(2)}, u32[]{:S(2)}) async-start(bf16[8,464,256]{2,1,0:T(8,128)(2,1)} %bitcast.26), calls=%async_computation.3 | async-start | bytes 3801088 | tf_op jit(solution)/shard_map/all_to_all | solution.py:606
  122.8 14.0 %copy-start.8 = (f32[2048,256]{1,0:T(8,128)S(1)}, f32[2048,256]{1,0:T(8,128)}, u32[]{:S(2)}) copy-start(f32[2048,256]{1,0:T(8,128)} %copy-done.7) | copy-start | bytes 6291460
  122.8 14.0 %copy-start.13 = (f32[2048,256]{1,0:T(8,128)S(1)}, f32[2048,256]{1,0:T(8,128)}, u32[]{:S(2)}) copy-start(f32[2048,256]{1,0:T(8,128)} %copy-done.11) | copy-start | bytes 6291460
  135.3 13.2 %copy-start.6 = (f32[2048,256]{1,0:T(8,128)S(1)}, f32[2048,256]{1,0:T(8,128)}, u32[]{:S(2)}) copy-start(f32[2048,256]{1,0:T(8,128)} %refs_0_.1) | copy-start | bytes 6291460
  137.9 30.1 %collective-permute-start.8 = (bf16[2048,256]{1,0:T(8,128)(2,1)}, bf16[2048,256]{1,0:T(8,128)(2,1)}, u32[]{:S(2)}, u32[]{:S(2)}) collective-permute-start(bf16[2048,256]{1,0:T(8,128)(2,1)} %get-tuple-element.79), channel_id=1, source_target_pairs={{0,8},{8,16},{16,24},{1,9},{9,17},{17,25},{2,10},{10,18},{18,26},{... | collective-permute-start | bytes 3145736 | tf_op jit(solution)/shard_map/ppermute | solution.py:649
  146.6 26.5 %collective-permute-start.9 = (bf16[2048,256]{1,0:T(8,128)(2,1)}, bf16[2048,256]{1,0:T(8,128)(2,1)}, u32[]{:S(2)}, u32[]{:S(2)}) collective-permute-start(bf16[2048,256]{1,0:T(8,128)(2,1)} %get-tuple-element.80), channel_id=1, source_target_pairs={{8,0},{16,8},{24,16},{9,1},{17,9},{25,17},{10,2},{18,10},{26,18},{... | collective-permute-start | bytes 3145736 | tf_op jit(solution)/shard_map/ppermute | solution.py:650

commit v2 on v1

--- a/solution.py
+++ b/solution.py
@@ -546,6 +546,53 @@
     )(*parts, in_hbm(up), in_hbm(down), *tokens)
 
 
+def finish_kernel(last_ref, up_from, down_from, volume_to, came_ref, sum_ref, sems):
+    lines = last_ref.shape[0]
+    tiles = sems.shape[1]
+    tile = lines // tiles
+
+    def copies(k):
+        at = pl.ds(k * tile, tile)
+        return (
+            pltpu.make_async_copy(up_from.at[at], came_ref.at[0, at], sems.at[0, k]),
+            pltpu.make_async_copy(down_from.at[at], came_ref.at[1, at], sems.at[1, k]),
+            pltpu.make_async_copy(sum_ref.at[at], volume_to.at[at], sems.at[2, k]),
+        )
+
+    for k in range(tiles):
+        up, down, _ = copies(k)
+        up.start()
+        down.start()
+    for k in range(tiles):
+        up, down, out = copies(k)
+        up.wait()
+        down.wait()
+        at = slice(k * tile, (k + 1) * tile)
+        came = came_ref[0, at, :].astype(F32) + came_ref[1, at, :].astype(F32)
+        sum_ref[at, :] = last_ref[at, :] + came
+        out.start()
+    for k in range(tiles):
+        copies(k)[2].wait()
+
+
+def finish(last, up, down):
+    hbm = pl.BlockSpec(memory_space=pltpu.HBM)
+    return pl.pallas_call(
+        finish_kernel,
+        out_shape=pltpu.HBM(last.shape, F32),
+        in_specs=[pl.BlockSpec(memory_space=pltpu.VMEM), hbm, hbm],
+        out_specs=hbm,
+        scratch_shapes=[
+            pltpu.VMEM((2,) + up.shape, BF16),
+            pltpu.VMEM(last.shape, F32),
+            pltpu.SemaphoreType.DMA((3, 4)),
+        ],
+        compiler_params=vmem_params(12),
+        cost_estimate=cost(1e6, 8e6),
+        name="finish",
+    )(last, in_hbm(up), in_hbm(down))
+
+
 def together(*values):
     return lax.optimization_barrier(values)
 
@@ -649,7 +696,7 @@
         up = lax.ppermute(up_send, "z", [(p, p + 1) for p in range(s)])
         down = lax.ppermute(down_send, "z", [(p, p - 1) for p in range(planes - s, planes)])
     last = lines_of(planes - 1, volume_in)
-    volume = last + up.astype(F32) + down.astype(F32)
+    volume = finish(last, up, down)
     return volume, evidence[:, 0]
 
 

time: 177 us -> 176 us (level)
  other arithmetic: 6.03 us -> 2.9 us
  Pallas kernels: 88.6 us -> 91 us
    add x1 -> x0, other arithmetic: 3.13 us -> none  [body(): volume = last + up.astype(F32) + down.astype(F32)]
    pallas_call x0 -> x1, Pallas kernels: none -> 2.51 us  [finish(): pl.pallas_call(finish_kernel, out_shape=pltpu.HBM(last.shape, F32), in_sp...]
  transfers between devices with their start and end apart: 15 -> 15, of which waited for: 6 -> 7; matrix products, arithmetic and copies ran while one was open for 2% -> 2% of each run, Pallas kernels for 50% -> 50%
where the time goes in v2:
time: 176 us
  Pallas kernels  91 us (52%)
  starting transfers between devices  53.5 us (30%)
  waiting for transfers between devices  20.1 us (11%)
  local copies, waits for them, and re-layouts  6.92 us (4%)
  other arithmetic  2.9 us (2%)
    pallas_call x4, Pallas kernels, partial_lines(): pl.pallas_call(functools.partial(gather_kernel, cap, pad, None if extra e...  50.9 us
    pallas_call x4, Pallas kernels, placed_rows(): pl.pallas_call(functools.partial(place_kernel, chunk, cap), grid=(1,), ou...  21.3 us
    all_to_all x4, starting transfers between devices, to_members(): lax.all_to_all(value.reshape(group, span, 2 * FX), ('x', 'slab'), 0, 0, t...  18 us
    ppermute x2, starting transfers between devices, body(): up = lax.ppermute(up_send, 'z', [(p, p + 1) for p in range(s)])  14.7 us
    pallas_call x1, Pallas kernels, weights_table(): pl.pallas_call(functools.partial(score_kernel, planes, inner), out_shape=...  9.2 us
    ppermute x2, waiting for transfers between devices, body(): up = lax.ppermute(up_send, 'z', [(p, p + 1) for p in range(s)])  9.01 us
    ppermute x1, starting transfers between devices, body(): lax.ppermute(short, 'z', sorted({(0, 1), (planes - 1, planes - 2)}))  5.73 us
    unnamed x39, local copies, waits for them, and re-layouts  5.59 us
  transfers between devices with their start and end apart: 15, of which 7 were waited for; matrix products, arithmetic and copies ran while one was open for 2% of the time, Pallas kernels for 50%

profile of v2, /device:TPU:0, one launch (start us, length us, event | category | flops | bytes accessed | tf_op | source)
XLA Modules:
  0.0 175.6 jit_solution(403152209939290688)
XLA Ops:
  1.7 3.0 %collective-permute-start = (bf16[2,32768]{1,0:T(2,128)(2,1)S(1)}, bf16[2,32768]{1,0:T(2,128)(2,1)S(1)}, u32[]{:S(2)}, u32[]{:S(2)}) collective-permute-start(bf16[2,32768]{1,0:T(2,128)(2,1)S(1)} %constant_dynamic-slice_fusion), channel_id=1, source_target_pairs={{0,4},{4,0},{1,5},{5,1},{2,6},{6,2},{3,7},{7,3},{8,12},{12,8},{9,1... | collective-permute-start | bytes 393224 | tf_op jit(solution)/shard_map/ppermute | solution.py:625
  5.4 4.7 %slots.1 = (s32[32,512]{1,0:T(8,128)S(1)}, f32[128,512]{1,0:T(8,128)S(1)}, f32[4096,128]{1,0:T(8,128)S(1)}, f32[4096,128]{1,0:T(8,128)S(1)}) custom-call(s32[16,512]{1,0:T(8,128)S(1)} %bitcast.24, s32[16,512]{1,0:T(8,128)} %line_from.1, bf16[16,65536]{1,0:T(8,128)(2,1)} %image_from.3), custom_call_target="tpu_custom_call" | custom-call | flops 3000000000 | bytes 12000000 | tf_op jit(solution)/shard_map/slots/pallas_call | solution.py:123
  10.4 1.6 collective-permute-start.1
  12.1 2.6 %collective-permute-start.2 = (bf16[4,32768]{1,0:T(4,128)(2,1)S(1)}, bf16[4,32768]{1,0:T(4,128)(2,1)}, u32[]{:S(2)}, u32[]{:S(2)}) collective-permute-start(bf16[4,32768]{1,0:T(4,128)(2,1)S(1)} %pad_maximum_fusion.1), channel_id=1, source_target_pairs={{0,16},{8,24},{16,0},{24,8},{1,17},{9,25},{17,1},{25,9},{2,18},{10... | collective-permute-start | bytes 786440 | tf_op jit(solution)/shard_map/ppermute | solution.py:641
  16.0 5.6 %place.5 = (bf16[3712,256]{1,0:T(8,128)(2,1)}, f32[8,128]{1,0:T(8,128)}) custom-call(s32[16384]{0:T(1024)S(1)} %bitcast.15, f32[128,512]{1,0:T(8,128)S(1)} %get-tuple-element.46.digit_ref, f32[4096,128]{1,0:T(8,128)S(1)} %get-tuple-element.47.real_ref, f32[4096,128]{1,0:T(8,128)S(1)} %get-tuple-element.48.imag_ref), custom_call_target="tpu_custom_call" | custom-call | flops 100000 | bytes 100000 | tf_op jit(solution)/shard_map/place/pallas_call | solution.py:201
  21.6 4.3 %all-to-all-start = ((bf16[8,464,256]{2,1,0:T(8,128)(2,1)}), bf16[8,464,256]{2,1,0:T(8,128)(2,1)}, u32[]{:S(2)}, u32[]{:S(2)}) async-start(bf16[8,464,256]{2,1,0:T(8,128)(2,1)} %bitcast.28), calls=%async_computation | async-start | bytes 3801088 | tf_op jit(solution)/shard_map/all_to_all | solution.py:653
  26.0 1.6 copy-done.2
  27.6 5.3 %place.4 = (bf16[3712,256]{1,0:T(8,128)(2,1)}, f32[8,128]{1,0:T(8,128)S(1)}) custom-call(s32[16384]{0:T(1024)S(1)} %bitcast.16, f32[128,512]{1,0:T(8,128)S(1)} %get-tuple-element.46.digit_ref, f32[4096,128]{1,0:T(8,128)S(1)} %get-tuple-element.47.real_ref, f32[4096,128]{1,0:T(8,128)S(1)} %copy-done.2), custom_call_target="tpu_custom_call" | custom-call | flops 100000 | bytes 100000 | tf_op jit(solution)/shard_map/place/pallas_call | solution.py:201
  33.0 2.6 %pad_maximum_fusion.near_ref = bf16[16,32768]{1,0:T(8,128)(2,1)} fusion(bf16[4,32768]{1,0:T(4,128)(2,1)} %collective-permute-done.3, bf16[4,32768]{1,0:T(4,128)(2,1)} %collective-permute-done.2, bf16[4,32768]{1,0:T(4,128)(2,1)S(1)} %collective-permute-done.1, bf16[4,32768]{1,0:T(4,128)(2,1)S(1)} %pad_maximum_fusion.1), kind=kLoop, calls=%fused_computation | loop fusion | flops 4194304 | bytes 2097152 | tf_op jit(solution)/shard_map/concatenate | solution.py:659
  36.1 2.5 %collective-permute-done.4.far_ref = bf16[16,32768]{1,0:T(8,128)(2,1)} collective-permute-done((bf16[16,32768]{1,0:T(8,128)(2,1)}, bf16[16,32768]{1,0:T(8,128)(2,1)}, u32[]{:S(2)}, u32[]{:S(2)}) %collective-permute-start.4) | collective-permute-done | bytes 1048608 | tf_op jit(solution)/shard_map/ppermute | solution.py:660
  38.6 9.2 %scores.1 = (f32[16,128]{1,0:T(8,128)S(1)}, f32[16,128]{1,0:T(8,128)S(1)}) custom-call(s32[1]{0:T(128)} %bitcast.half_ref, f32[4,256]{1,0:T(4,128)S(1)} %copy-done.10, bf16[16,65536]{1,0:T(8,128)(2,1)} %image_from.3, bf16[16,32768]{1,0:T(8,128)(2,1)} %pad_maximum_fusion.near_ref, bf16[16,32768]{1,0:T(8,128)(2,1)} %collective-permute-done.4.far_ref, ...), custom_call_target="tpu_custom_call" | custom-call | flops 1000000000 | bytes 5000000 | tf_op jit(solution)/shard_map/scores/pallas_call | solution.py:351
  47.8 1.8 %all-to-all-done = bf16[8,464,256]{2,1,0:T(8,128)(2,1)} async-done(((bf16[8,464,256]{2,1,0:T(8,128)(2,1)}), bf16[8,464,256]{2,1,0:T(8,128)(2,1)}, u32[]{:S(2)}, u32[]{:S(2)}) %all-to-all-start) | async-done | bytes 1900576 | tf_op jit(solution)/shard_map/all_to_all | solution.py:653
  50.2 3.3 %all-to-all-start.1 = ((f32[8,16,128]{2,1,0:T(8,128)}), f32[8,16,128]{2,1,0:T(8,128)S(1)}, u32[]{:S(2)}, u32[]{:S(2)}) async-start(f32[8,16,128]{2,1,0:T(8,128)} %broadcast_in_dim.2), calls=%async_computation.1 | async-start | bytes 131072 | tf_op jit(solution)/shard_map/all_to_all | solution.py:669
  53.6 1.6 copy-done.3
  55.1 5.1 %place.6 = (bf16[3712,256]{1,0:T(8,128)(2,1)}, f32[8,128]{1,0:T(8,128)S(1)}) custom-call(s32[16384]{0:T(1024)S(1)} %bitcast.17, f32[128,512]{1,0:T(8,128)S(1)} %get-tuple-element.46.digit_ref, f32[4096,128]{1,0:T(8,128)S(1)} %get-tuple-element.47.real_ref, f32[4096,128]{1,0:T(8,128)S(1)} %copy-done.3), custom_call_target="tpu_custom_call" | custom-call | flops 100000 | bytes 100000 | tf_op jit(solution)/shard_map/place/pallas_call | solution.py:201
  60.3 4.7 %all-to-all-start.2 = ((bf16[8,464,256]{2,1,0:T(8,128)(2,1)}), bf16[8,464,256]{2,1,0:T(8,128)(2,1)}, u32[]{:S(2)}, u32[]{:S(2)}) async-start(bf16[8,464,256]{2,1,0:T(8,128)(2,1)} %bitcast.25), calls=%async_computation.2 | async-start | bytes 3801088 | tf_op jit(solution)/shard_map/all_to_all | solution.py:653
  65.0 13.5 %lines.5 = (f32[2048,256]{1,0:T(8,128)S(1)}, bf16[2048,256]{1,0:T(8,128)(2,1)}) custom-call(bf16[3712,256]{1,0:T(8,128)(2,1)} %bitcast.2.row_ref, f32[128,128]{1,0:T(8,128)S(1)} %bitcast.19, bf16[144,256]{1,0:T(8,128)(2,1)S(1)} %copy-done.9, bf16[8,128,128]{2,1,0:T(8,128)(2,1)S(1)} %copy-done.5), custom_call_target="tpu_custom_call" | custom-call | flops 1000000 | bytes 100000 | tf_op jit(solution)/shard_map/lines/pallas_call | solution.py:471
  78.6 5.7 %collective-permute-start.5 = (bf16[2048,256]{1,0:T(8,128)(2,1)}, bf16[2048,256]{1,0:T(8,128)(2,1)}, u32[]{:S(2)}, u32[]{:S(2)}) collective-permute-start(bf16[2048,256]{1,0:T(8,128)(2,1)} %get-tuple-element.74), channel_id=1, source_target_pairs={{0,8},{24,16},{1,9},{25,17},{2,10},{26,18},{3,11},{27,19},{4,12},{... | collective-permute-start | bytes 3145736 | tf_op jit(solution)/shard_map/ppermute | solution.py:685
  84.3 5.4 %place.7 = (bf16[3712,256]{1,0:T(8,128)(2,1)}, f32[8,128]{1,0:T(8,128)S(1)}) custom-call(s32[16384]{0:T(1024)S(1)} %bitcast.18, f32[128,512]{1,0:T(8,128)S(1)} %get-tuple-element.46.digit_ref, f32[4096,128]{1,0:T(8,128)S(1)} %get-tuple-element.47.real_ref, f32[4096,128]{1,0:T(8,128)S(1)} %copy-done.4), custom_call_target="tpu_custom_call" | custom-call | flops 100000 | bytes 100000 | tf_op jit(solution)/shard_map/place/pallas_call | solution.py:201
  89.7 4.4 %all-to-all-start.4 = ((bf16[8,464,256]{2,1,0:T(8,128)(2,1)}), bf16[8,464,256]{2,1,0:T(8,128)(2,1)}, u32[]{:S(2)}, u32[]{:S(2)}) async-start(bf16[8,464,256]{2,1,0:T(8,128)(2,1)} %bitcast.27), calls=%async_computation.4 | async-start | bytes 3801088 | tf_op jit(solution)/shard_map/all_to_all | solution.py:653
  94.1 12.5 %lines.4.refs_1_ = f32[2048,256]{1,0:T(8,128)S(1)} custom-call(bf16[3712,256]{1,0:T(8,128)(2,1)} %bitcast.5.row_ref, f32[128,128]{1,0:T(8,128)S(1)} %bitcast.20, bf16[144,256]{1,0:T(8,128)(2,1)S(1)} %copy-done.9, bf16[8,128,128]{2,1,0:T(8,128)(2,1)S(1)} %copy-done.5), custom_call_target="tpu_custom_call" | custom-call | flops 1000000 | bytes 100000 | tf_op jit(solution)/shard_map/lines/pallas_call | solution.py:471
  108.2 6.1 %collective-permute-start.6 = (bf16[2048,256]{1,0:T(8,128)(2,1)}, bf16[2048,256]{1,0:T(8,128)(2,1)}, u32[]{:S(2)}, u32[]{:S(2)}) collective-permute-start(bf16[2048,256]{1,0:T(8,128)(2,1)} %get-tuple-element.77), channel_id=1, source_target_pairs={{0,8},{8,16},{1,9},{9,17},{2,10},{10,18},{3,11},{11,19},{4,12},{12... | collective-permute-start | bytes 3145736 | tf_op jit(solution)/shard_map/ppermute | solution.py:696
  114.3 1.6 collective-permute-start.7
  115.9 1.7 all-to-all-done.4
  117.6 4.5 %all-to-all-start.3 = ((bf16[8,464,256]{2,1,0:T(8,128)(2,1)}), bf16[8,464,256]{2,1,0:T(8,128)(2,1)}, u32[]{:S(2)}, u32[]{:S(2)}) async-start(bf16[8,464,256]{2,1,0:T(8,128)(2,1)} %bitcast.26), calls=%async_computation.3 | async-start | bytes 3801088 | tf_op jit(solution)/shard_map/all_to_all | solution.py:653
  122.2 12.5 %lines.7.refs_2_ = f32[2048,256]{1,0:T(8,128)S(1)} custom-call(bf16[3712,256]{1,0:T(8,128)(2,1)} %bitcast.9.row_ref, f32[128,128]{1,0:T(8,128)S(1)} %bitcast.21, bf16[144,256]{1,0:T(8,128)(2,1)S(1)} %copy-done.9, bf16[8,128,128]{2,1,0:T(8,128)(2,1)S(1)} %copy-done.5), custom_call_target="tpu_custom_call" | custom-call | flops 1000000 | bytes 100000 | tf_op jit(solution)/shard_map/lines/pallas_call | solution.py:471
  134.7 1.8 %collective-permute-done.6.refs_3_ = bf16[2048,256]{1,0:T(8,128)(2,1)} collective-permute-done((bf16[2048,256]{1,0:T(8,128)(2,1)}, bf16[2048,256]{1,0:T(8,128)(2,1)}, u32[]{:S(2)}, u32[]{:S(2)}) %collective-permute-start.6) | collective-permute-done | bytes 1048608 | tf_op jit(solution)/shard_map/ppermute | solution.py:696
  137.7 8.6 %collective-permute-start.8 = (bf16[2048,256]{1,0:T(8,128)(2,1)}, bf16[2048,256]{1,0:T(8,128)(2,1)}, u32[]{:S(2)}, u32[]{:S(2)}) collective-permute-start(bf16[2048,256]{1,0:T(8,128)(2,1)} %get-tuple-element.79), channel_id=1, source_target_pairs={{0,8},{8,16},{16,24},{1,9},{9,17},{17,25},{2,10},{10,18},{18,26},{... | collective-permute-start | bytes 3145736 | tf_op jit(solution)/shard_map/ppermute | solution.py:696
  148.3 12.4 %lines.6.last_ref = f32[2048,256]{1,0:T(8,128)S(1)} custom-call(bf16[3712,256]{1,0:T(8,128)(2,1)} %bitcast.7.row_ref, f32[128,128]{1,0:T(8,128)S(1)} %bitcast.22, bf16[144,256]{1,0:T(8,128)(2,1)S(1)} %copy-done.9, bf16[8,128,128]{2,1,0:T(8,128)(2,1)S(1)} %copy-done.5, f32[2048,256]{1,0:T(8,128)S(1)} %copy-done.6), custom_call_target="tpu_custom_call" | custom-call | flops 1000000 | bytes 100000 | tf_op jit(solution)/shard_map/lines/pallas_call | solution.py:471
  160.6 7.2 %collective-permute-done.8.up_from = bf16[2048,256]{1,0:T(8,128)(2,1)} collective-permute-done((bf16[2048,256]{1,0:T(8,128)(2,1)}, bf16[2048,256]{1,0:T(8,128)(2,1)}, u32[]{:S(2)}, u32[]{:S(2)}) %collective-permute-start.8) | collective-permute-done | bytes 1048608 | tf_op jit(solution)/shard_map/ppermute | solution.py:696
  167.8 5.1 %collective-permute-done.9.down_from = bf16[2048,256]{1,0:T(8,128)(2,1)} collective-permute-done((bf16[2048,256]{1,0:T(8,128)(2,1)}, bf16[2048,256]{1,0:T(8,128)(2,1)}, u32[]{:S(2)}, u32[]{:S(2)}) %collective-permute-start.9) | collective-permute-done | bytes 1048608 | tf_op jit(solution)/shard_map/ppermute | solution.py:697
  172.9 2.5 %finish.1 = f32[2048,256]{1,0:T(8,128)} custom-call(f32[2048,256]{1,0:T(8,128)S(1)} %lines.6.last_ref, bf16[2048,256]{1,0:T(8,128)(2,1)} %collective-permute-done.8.up_from, bf16[2048,256]{1,0:T(8,128)(2,1)} %collective-permute-done.9.down_from), custom_call_target="tpu_custom_call" | custom-call | flops 1000000 | bytes 8000000 | tf_op jit(solution)/shard_map/finish/pallas_call | solution.py:580
  (55 shorter events, 9.4 us)
Async XLA Ops:
  0.6 1.0 copy-start
  1.7 8.5 %collective-permute-start = (bf16[2,32768]{1,0:T(2,128)(2,1)S(1)}, bf16[2,32768]{1,0:T(2,128)(2,1)S(1)}, u32[]{:S(2)}, u32[]{:S(2)}) collective-permute-start(bf16[2,32768]{1,0:T(2,128)(2,1)S(1)} %constant_dynamic-slice_fusion), channel_id=1, source_target_pairs={{0,4},{4,0},{1,5},{5,1},{2,6},{6,2},{3,7},{7,3},{8,12},{12,8},{9,1... | collective-permute-start | bytes 393224 | tf_op jit(solution)/shard_map/ppermute | solution.py:625
  10.1 11.5 %copy-start.1 = (f32[4096,128]{1,0:T(8,128)}, f32[4096,128]{1,0:T(8,128)S(1)}, u32[]{:S(2)}) copy-start(f32[4096,128]{1,0:T(8,128)S(1)} %get-tuple-element.48.imag_ref) | copy-start | bytes 6291460
  10.4 22.5 %collective-permute-start.1 = (bf16[4,32768]{1,0:T(4,128)(2,1)S(1)}, bf16[4,32768]{1,0:T(4,128)(2,1)S(1)}, u32[]{:S(2)}, u32[]{:S(2)}) collective-permute-start(bf16[4,32768]{1,0:T(4,128)(2,1)S(1)} %pad_maximum_fusion.1), channel_id=1, source_target_pairs={{0,8},{8,16},{16,24},{24,0},{1,9},{9,17},{17,25},{25,1},{2,10},{10... | collective-permute-start | bytes 786440 | tf_op jit(solution)/shard_map/ppermute | solution.py:641
  12.1 20.9 %collective-permute-start.2 = (bf16[4,32768]{1,0:T(4,128)(2,1)S(1)}, bf16[4,32768]{1,0:T(4,128)(2,1)}, u32[]{:S(2)}, u32[]{:S(2)}) collective-permute-start(bf16[4,32768]{1,0:T(4,128)(2,1)S(1)} %pad_maximum_fusion.1), channel_id=1, source_target_pairs={{0,16},{8,24},{16,0},{24,8},{1,17},{9,25},{17,1},{25,9},{2,18},{10... | collective-permute-start | bytes 786440 | tf_op jit(solution)/shard_map/ppermute | solution.py:641
  14.6 18.3 %collective-permute-start.3 = (bf16[4,32768]{1,0:T(4,128)(2,1)S(1)}, bf16[4,32768]{1,0:T(4,128)(2,1)}, u32[]{:S(2)}, u32[]{:S(2)}) collective-permute-start(bf16[4,32768]{1,0:T(4,128)(2,1)S(1)} %pad_maximum_fusion.1), channel_id=1, source_target_pairs={{0,24},{8,0},{16,8},{24,16},{1,25},{9,1},{17,9},{25,17},{2,26},{10... | collective-permute-start | bytes 786440 | tf_op jit(solution)/shard_map/ppermute | solution.py:641
  21.6 27.9 %all-to-all-start = ((bf16[8,464,256]{2,1,0:T(8,128)(2,1)}), bf16[8,464,256]{2,1,0:T(8,128)(2,1)}, u32[]{:S(2)}, u32[]{:S(2)}) async-start(bf16[8,464,256]{2,1,0:T(8,128)(2,1)} %bitcast.28), calls=%async_computation | async-start | bytes 3801088 | tf_op jit(solution)/shard_map/all_to_all | solution.py:653
  26.0 1.6 copy-start.2
  32.9 3.0 %copy-start.14 = (s32[16,2]{0,1:T(2,128)S(1)}, s32[16,2]{0,1:T(2,128)}, u32[]{:S(2)}) copy-start(s32[16,2]{0,1:T(2,128)} %param.16) | copy-start | bytes 388
  32.9 3.0 %copy-start.15 = (s32[16,2]{0,1:T(2,128)S(1)}, s32[16,2]{0,1:T(2,128)}, u32[]{:S(2)}) copy-start(s32[16,2]{0,1:T(2,128)} %param.17) | copy-start | bytes 388
  32.9 3.1 %copy-start.16 = (s32[16,2]{0,1:T(2,128)S(1)}, s32[16,2]{0,1:T(2,128)}, u32[]{:S(2)}) copy-start(s32[16,2]{0,1:T(2,128)} %param.19) | copy-start | bytes 388
  32.9 5.7 %copy-start.10 = (f32[4,256]{1,0:T(4,128)S(1)}, f32[4,256]{1,0:T(4,128)}, u32[]{:S(2)}) copy-start(f32[4,256]{1,0:T(4,128)} %constant.26.clone.turn_ref) | copy-start | bytes 12292
  35.6 3.0 %collective-permute-start.4 = (bf16[16,32768]{1,0:T(8,128)(2,1)}, bf16[16,32768]{1,0:T(8,128)(2,1)}, u32[]{:S(2)}, u32[]{:S(2)}) collective-permute-start(bf16[16,32768]{1,0:T(8,128)(2,1)} %pad_maximum_fusion.near_ref), channel_id=1, source_target_pairs={{0,1},{1,0},{2,3},{3,2},{4,5},{5,4},{6,7},{7,6},{8,9},{9,8},{10,11... | collective-permute-start | bytes 3145736 | tf_op jit(solution)/shard_map/ppermute | solution.py:660
  50.2 10.1 %all-to-all-start.1 = ((f32[8,16,128]{2,1,0:T(8,128)}), f32[8,16,128]{2,1,0:T(8,128)S(1)}, u32[]{:S(2)}, u32[]{:S(2)}) async-start(f32[8,16,128]{2,1,0:T(8,128)} %broadcast_in_dim.2), calls=%async_computation.1 | async-start | bytes 131072 | tf_op jit(solution)/shard_map/all_to_all | solution.py:669
  53.5 1.6 copy-start.3
  60.2 4.8 %copy-start.5 = (bf16[8,128,128]{2,1,0:T(8,128)(2,1)S(1)}, bf16[8,128,128]{2,1,0:T(8,128)(2,1)}, u32[]{:S(2)}) copy-start(bf16[8,128,128]{2,1,0:T(8,128)(2,1)} %mats_ref.7) | copy-start | bytes 786436
  60.2 4.8 %copy-start.9 = (bf16[144,256]{1,0:T(8,128)(2,1)S(1)}, bf16[144,256]{1,0:T(8,128)(2,1)}, u32[]{:S(2)}) copy-start(bf16[144,256]{1,0:T(8,128)(2,1)} %constant.27.clone.wave_ref) | copy-start | bytes 221188
  60.3 29.4 %all-to-all-start.2 = ((bf16[8,464,256]{2,1,0:T(8,128)(2,1)}), bf16[8,464,256]{2,1,0:T(8,128)(2,1)}, u32[]{:S(2)}, u32[]{:S(2)}) async-start(bf16[8,464,256]{2,1,0:T(8,128)(2,1)} %bitcast.25), calls=%async_computation.2 | async-start | bytes 3801088 | tf_op jit(solution)/shard_map/all_to_all | solution.py:653
  65.0 19.3 %copy-start.4 = (f32[4096,128]{1,0:T(8,128)S(1)}, f32[4096,128]{1,0:T(8,128)}, u32[]{:S(2)}) copy-start(f32[4096,128]{1,0:T(8,128)} %copy-done.1) | copy-start | bytes 6291460
  78.6 11.1 %copy-start.11 = (f32[2048,256]{1,0:T(8,128)}, f32[2048,256]{1,0:T(8,128)S(1)}, u32[]{:S(2)}) copy-start(f32[2048,256]{1,0:T(8,128)S(1)} %get-tuple-element.69.refs_0_) | copy-start | bytes 6291460
  78.6 28.1 %collective-permute-start.5 = (bf16[2048,256]{1,0:T(8,128)(2,1)}, bf16[2048,256]{1,0:T(8,128)(2,1)}, u32[]{:S(2)}, u32[]{:S(2)}) collective-permute-start(bf16[2048,256]{1,0:T(8,128)(2,1)} %get-tuple-element.74), channel_id=1, source_target_pairs={{0,8},{24,16},{1,9},{25,17},{2,10},{26,18},{3,11},{27,19},{4,12},{... | collective-permute-start | bytes 3145736 | tf_op jit(solution)/shard_map/ppermute | solution.py:685
  89.7 28.0 %all-to-all-start.4 = ((bf16[8,464,256]{2,1,0:T(8,128)(2,1)}), bf16[8,464,256]{2,1,0:T(8,128)(2,1)}, u32[]{:S(2)}, u32[]{:S(2)}) async-start(bf16[8,464,256]{2,1,0:T(8,128)(2,1)} %bitcast.27), calls=%async_computation.4 | async-start | bytes 3801088 | tf_op jit(solution)/shard_map/all_to_all | solution.py:653
  94.0 12.6 %copy-start.12 = (f32[2048,256]{1,0:T(8,128)S(1)}, f32[2048,256]{1,0:T(8,128)}, u32[]{:S(2)}) copy-start(f32[2048,256]{1,0:T(8,128)} %copy-done.11) | copy-start | bytes 6291460
  106.6 1.7 copy-start.7
  108.2 28.4 %collective-permute-start.6 = (bf16[2048,256]{1,0:T(8,128)(2,1)}, bf16[2048,256]{1,0:T(8,128)(2,1)}, u32[]{:S(2)}, u32[]{:S(2)}) collective-permute-start(bf16[2048,256]{1,0:T(8,128)(2,1)} %get-tuple-element.77), channel_id=1, source_target_pairs={{0,8},{8,16},{1,9},{9,17},{2,10},{10,18},{3,11},{11,19},{4,12},{12... | collective-permute-start | bytes 3145736 | tf_op jit(solution)/shard_map/ppermute | solution.py:696
  114.3 22.3 %collective-permute-start.7 = (bf16[2048,256]{1,0:T(8,128)(2,1)}, bf16[2048,256]{1,0:T(8,128)(2,1)}, u32[]{:S(2)}, u32[]{:S(2)}) collective-permute-start(bf16[2048,256]{1,0:T(8,128)(2,1)} %get-tuple-element.78), channel_id=1, source_target_pairs={{16,8},{24,16},{17,9},{25,17},{18,10},{26,18},{19,11},{27,19},{20,... | collective-permute-start | bytes 3145736 | tf_op jit(solution)/shard_map/ppermute | solution.py:697
  117.6 30.6 %all-to-all-start.3 = ((bf16[8,464,256]{2,1,0:T(8,128)(2,1)}), bf16[8,464,256]{2,1,0:T(8,128)(2,1)}, u32[]{:S(2)}, u32[]{:S(2)}) async-start(bf16[8,464,256]{2,1,0:T(8,128)(2,1)} %bitcast.26), calls=%async_computation.3 | async-start | bytes 3801088 | tf_op jit(solution)/shard_map/all_to_all | solution.py:653
  122.2 14.4 %copy-start.8 = (f32[2048,256]{1,0:T(8,128)S(1)}, f32[2048,256]{1,0:T(8,128)}, u32[]{:S(2)}) copy-start(f32[2048,256]{1,0:T(8,128)} %copy-done.7) | copy-start | bytes 6291460
  122.2 14.4 %copy-start.13 = (f32[2048,256]{1,0:T(8,128)S(1)}, f32[2048,256]{1,0:T(8,128)}, u32[]{:S(2)}) copy-start(f32[2048,256]{1,0:T(8,128)} %copy-done.11) | copy-start | bytes 6291460
  134.7 13.6 %copy-start.6 = (f32[2048,256]{1,0:T(8,128)S(1)}, f32[2048,256]{1,0:T(8,128)}, u32[]{:S(2)}) copy-start(f32[2048,256]{1,0:T(8,128)} %refs_0_.1) | copy-start | bytes 6291460
  137.7 30.1 %collective-permute-start.8 = (bf16[2048,256]{1,0:T(8,128)(2,1)}, bf16[2048,256]{1,0:T(8,128)(2,1)}, u32[]{:S(2)}, u32[]{:S(2)}) collective-permute-start(bf16[2048,256]{1,0:T(8,128)(2,1)} %get-tuple-element.79), channel_id=1, source_target_pairs={{0,8},{8,16},{16,24},{1,9},{9,17},{17,25},{2,10},{10,18},{18,26},{... | collective-permute-start | bytes 3145736 | tf_op jit(solution)/shard_map/ppermute | solution.py:696
  146.4 26.5 %collective-permute-start.9 = (bf16[2048,256]{1,0:T(8,128)(2,1)}, bf16[2048,256]{1,0:T(8,128)(2,1)}, u32[]{:S(2)}, u32[]{:S(2)}) collective-permute-start(bf16[2048,256]{1,0:T(8,128)(2,1)} %get-tuple-element.80), channel_id=1, source_target_pairs={{8,0},{16,8},{24,16},{9,1},{17,9},{25,17},{10,2},{18,10},{26,18},{... | collective-permute-start | bytes 3145736 | tf_op jit(solution)/shard_map/ppermute | solution.py:697
